TPU v7x, 512 devices: a whole 4x8x8 slice. The times are simulated.
512 devices in a mesh: seq: 32 (over x, z), head: 16 (over y, core).
Axes of the slice: x: 4, y: 8, z: 8, core: 2. Of those that a mesh axis runs over, the one named last changes fastest.
Arguments:
- query_rows: float32 [16384, 4096], P('seq', 'head'), may hold values from -128 to 128
- key_rows: float32 [16384, 4096], P('seq', 'head'), may hold values from -128 to 128
- value_rows: float32 [16384, 4096], P('seq', 'head'), may hold values from -6 to 6
- teacher_out: float32 [16384, 4096], P(('seq', 'head')), may hold values from -6 to 6
- query_map: float32 [16, 256, 256], P('head'), may hold values from -1 to 1
- key_map: float32 [16, 256, 256], P('head'), may hold values from -1 to 1
- block_map: int32 [32, 32], replicated, may hold values from 0 to 1023, as said below
Outputs:
- grad_query_map: float32 [16, 256, 256], P('head', 'seq')
- grad_key_map: float32 [16, 256, 256], P('head', 'seq')
Inputs may be any that keep to these rules, and one draw needn't show every extreme that they name: `block_map`: row d lists, slot by slot, the sequence blocks whose teacher rows storage row group d holds (storage block d * 32 + j). Sequence block b belongs to owner b // 32. Every row names exactly one block of each owner, and every block appears exactly once in the table.
All inputs are finite; a program needn't handle non-finite values.
Results may differ from a plain program's by a relative error of at most 0.00035.
Values sent between devices are 32-bit elements; how exact they have to be, the bound alone decides.
No kernel may reach another device: no remote copies, remote signals or barrier semaphores. Data moves between devices by JAX's collectives and lax.ppermute only.
A program may use at most 128 MiB of HBM per device.

v0:
```python
import jax
import jax.numpy as jnp
from jax import lax
from jax.sharding import PartitionSpec as P

exact_prec = lax.Precision.HIGHEST


def prefix(value, axis, join, neutral, backward):
    count, mine = (lax.axis_size(axis), lax.axis_index(axis))
    pieces = jax.tree.map(lambda part: lax.all_gather(part, axis), value)
    if backward:
        pieces = jax.tree.map(lambda part: part[::-1], pieces)
        mine = count - 1 - mine
    total = jax.tree.map(
        lambda part, zero: jnp.full_like(part, 0) + jnp.asarray(zero, part.dtype), value, neutral
    )

    def step(position, total):
        longer = join(total, jax.tree.map(lambda part: part[position], pieces))
        return jax.tree.map(lambda new, old: jnp.where(position < mine, new, old), longer, total)

    return lax.fori_loop(0, count - 1, step, total)


def back_pair(first_half, second_half, grad_feat, half_feat):
    grad_first = grad_feat[..., :half_feat]
    grad_second = grad_feat[..., half_feat:]
    lead = first_half * (grad_first - jnp.sum(first_half * grad_first, axis=-1, keepdims=True))
    trail = second_half * (grad_second - jnp.sum(second_half * grad_second, axis=-1, keepdims=True))
    return lead - trail


def add_pair(earlier, later_one):
    return (earlier[0] + later_one[0], earlier[1] + later_one[1])


def relay_teacher(teacher_out, block_map):
    gathered = lax.all_to_all(teacher_out, "head", split_axis=1, concat_axis=0, tiled=True)
    seq_count = lax.axis_size("seq")
    position = lax.axis_index("seq")
    columns = gathered.shape[1]
    block_rows = gathered.shape[0] // seq_count
    blocks = gathered.reshape(seq_count, block_rows, columns)
    slot_ids = lax.dynamic_index_in_dim(block_map, position, 0, keepdims=False)
    owner_ids = slot_ids // seq_count
    ladder = jnp.arange(seq_count, dtype=jnp.int32)
    to_owner = (owner_ids[None, :] == ladder[:, None]).astype(jnp.float32)
    by_owner = jnp.einsum("oj,jrc->orc", to_owner, blocks, precision=exact_prec)
    arrived = lax.all_to_all(by_owner, "seq", split_axis=0, concat_axis=0, tiled=True)
    own_mask = block_map // seq_count == position
    within = jnp.sum(jnp.where(own_mask, block_map % seq_count, 0), axis=1)
    placing = (within[None, :] == ladder[:, None]).astype(jnp.float32)
    placed = jnp.einsum("is,src->irc", placing, arrived, precision=exact_prec)
    return placed.reshape(seq_count * block_rows, columns)


def per_device(query_rows, key_rows, value_rows, teacher_out, query_map, key_map, block_map):
    tokens = query_rows.shape[0]
    local_heads = query_map.shape[0]
    head_width = query_map.shape[1]
    half_feat = query_map.shape[2]
    queries = query_rows.reshape(tokens, local_heads, head_width).transpose(1, 0, 2)
    keys_h = key_rows.reshape(tokens, local_heads, head_width).transpose(1, 0, 2)
    values_h = value_rows.reshape(tokens, local_heads, head_width).transpose(1, 0, 2)
    pre_q = jnp.einsum("hte,hef->htf", queries, query_map, precision=exact_prec)
    pre_k = jnp.einsum("hte,hef->htf", keys_h, key_map, precision=exact_prec)
    first_q = jax.nn.softmax(pre_q, axis=-1)
    second_q = jax.nn.softmax(-pre_q, axis=-1)
    first_k = jax.nn.softmax(pre_k, axis=-1)
    second_k = jax.nn.softmax(-pre_k, axis=-1)
    feat_q = jnp.concatenate([first_q, second_q], axis=-1)
    feat_k = jnp.concatenate([first_k, second_k], axis=-1)
    own_state = jnp.einsum("htf,hte->hfe", feat_k, values_h, precision=exact_prec)
    own_norm = jnp.sum(feat_k, axis=1)
    zero_pair = (jnp.zeros_like(own_state), jnp.zeros_like(own_norm))
    prev_state, prev_norm = prefix((own_state, own_norm), "seq", add_pair, zero_pair, False)
    ladder = jnp.arange(tokens, dtype=jnp.int32)
    causal = (ladder[:, None] >= ladder[None, :]).astype(jnp.float32)
    scores = jnp.einsum("htf,hsf->hts", feat_q, feat_k, precision=exact_prec) * causal
    numerator = jnp.einsum("hts,hse->hte", scores, values_h, precision=exact_prec)
    numerator = numerator + jnp.einsum("htf,hfe->hte", feat_q, prev_state, precision=exact_prec)
    raw_sum = jnp.sum(scores, axis=-1) + jnp.einsum(
        "htf,hf->ht", feat_q, prev_norm, precision=exact_prec
    )
    divisor = jnp.maximum(raw_sum, 1.0)
    student = numerator / divisor[..., None]
    teacher_rows = relay_teacher(teacher_out, block_map)
    teacher = teacher_rows.reshape(tokens, local_heads, head_width).transpose(1, 0, 2)
    mismatch = student - teacher
    grad_num = mismatch / divisor[..., None]
    grad_div = jnp.where(raw_sum > 1.0, -jnp.sum(mismatch * student, axis=-1) / divisor, 0.0)
    own_back = jnp.einsum("htf,hte->hfe", feat_q, grad_num, precision=exact_prec)
    own_back_norm = jnp.einsum("ht,htf->hf", grad_div, feat_q, precision=exact_prec)
    next_state, next_norm = prefix((own_back, own_back_norm), "seq", add_pair, zero_pair, True)
    weights = (
        jnp.einsum("hte,hse->hts", grad_num, values_h, precision=exact_prec) + grad_div[..., None]
    ) * causal
    grad_fq = jnp.einsum("hts,hsf->htf", weights, feat_k, precision=exact_prec)
    grad_fq = grad_fq + jnp.einsum("hte,hfe->htf", grad_num, prev_state, precision=exact_prec)
    grad_fq = grad_fq + grad_div[..., None] * prev_norm[:, None, :]
    grad_fk = jnp.einsum("hts,htf->hsf", weights, feat_q, precision=exact_prec)
    grad_fk = grad_fk + jnp.einsum("hse,hfe->hsf", values_h, next_state, precision=exact_prec)
    grad_fk = grad_fk + next_norm[:, None, :]
    grad_pq = back_pair(first_q, second_q, grad_fq, half_feat)
    grad_pk = back_pair(first_k, second_k, grad_fk, half_feat)
    term_q = jnp.einsum("hte,htf->ehf", queries, grad_pq, precision=exact_prec)
    term_k = jnp.einsum("hte,htf->ehf", keys_h, grad_pk, precision=exact_prec)
    summed = lax.psum_scatter(
        jnp.stack([term_q, term_k], axis=1), "seq", scatter_dimension=0, tiled=True
    )
    grad_query = summed[:, 0].transpose(1, 0, 2)
    grad_key = summed[:, 1].transpose(1, 0, 2)
    return (grad_query, grad_key)


def solution(mesh):
    placed = (
        P("seq", "head"),
        P("seq", "head"),
        P("seq", "head"),
        P(("seq", "head"), None),
        P("head", None, None),
        P("head", None, None),
        P(),
    )
    return jax.shard_map(
        per_device,
        mesh=mesh,
        in_specs=placed,
        out_specs=(P("head", "seq", None), P("head", "seq", None)),
        check_vma=False,
    )
```

profile of v0, /device:TPU:16, one launch (start us, length us, event | category | flops | bytes accessed | tf_op | source)
XLA Modules:
  0.0 580.8 jit_solution(12528518958974841820)
XLA Ops:
  7.2 1.8 fusion.73
  9.1 1.8 fusion.74
  11.6 1.8 fusion.9
  13.4 1.9 copy.50
  15.3 9.1 %all-to-all-start = ((f32[32,16,256]{2,0,1:T(8,128)}), f32[32,16,256]{2,0,1:T(8,128)S(1)}, u32[]{:S(2)}, u32[]{:S(2)}) async-start(f32[32,16,256]{2,0,1:T(8,128)} %bitcast.151), calls=%async_computation | async-start | bytes 1048576 | tf_op jit(solution)/shard_map/all_to_all | solution.py:39
  25.0 14.2 %all-to-all-done = f32[32,16,256]{2,0,1:T(8,128)S(1)} async-done(((f32[32,16,256]{2,0,1:T(8,128)}), f32[32,16,256]{2,0,1:T(8,128)S(1)}, u32[]{:S(2)}, u32[]{:S(2)}) %all-to-all-start) | async-done | bytes 524320 | tf_op jit(solution)/shard_map/all_to_all | solution.py:39
  41.1 11.6 %all-to-all-start.1 = ((f32[32,16,256]{2,1,0:T(8,128)}), f32[32,16,256]{2,1,0:T(8,128)}, u32[]{:S(2)}, u32[]{:S(2)}) async-start(f32[32,16,256]{2,1,0:T(8,128)} %copy.34), calls=%async_computation.1 | async-start | bytes 1048576 | tf_op jit(solution)/shard_map/all_to_all | solution.py:50
  53.0 61.2 %all-gather.4 = f32[32,1,512]{2,1,0:T(1,128)S(1)} all-gather(f32[1,1,512]{2,1,0:T(1,128)S(1)} %bitcast.160), channel_id=3, replica_groups=mesh['seq'=32,'head'=16] {'seq'}, dimensions={0}, use_global_device_ids=true | all-gather | bytes 67584 | tf_op jit(solution)/shard_map/all_gather | solution.py:11
  115.1 1.9 fusion.75
  117.0 1.9 fusion.76
  118.9 1.7 fusion.17
  121.7 2.1 copy.37
  123.8 49.7 %all-gather.9.cloned.1.call-done = f32[16384,256]{1,0:T(8,128)} async-done(((f32[512,256]{1,0:T(8,128)}), f32[16384,256]{1,0:T(8,128)}) %all-gather.9.cloned.1.call-update) | async-done | bytes 16777232 | tf_op jit(solution)/shard_map/all_gather | solution.py:11
  173.5 38.6 %while.32 = (s32[]{:T(128)}, f32[1,512,256]{2,1,0:T(8,128)S(1)}, f32[1,512]{1,0:T(1,128)S(1)}, s32[]{:T(128)}, f32[32,1,512,256]{3,2,1,0:T(8,128)}, /*index=5*/f32[32,1,512]{2,1,0:T(1,128)S(1)}, s32[]{:T(128)}, s32[]{:T(128)}) while((s32[]{:T(128)}, f32[1,512,256]{2,1,0:T(8,128)S(1)}, f32[1,512]{1,0:T(1,128)S(1)}, s32[]{:T(128)}, ...), condition=%wide.region_10.11_spmd.clone, body=%wide.region_9.10_spmd.clone.sunk | while | flops 394756 | bytes 1579123 | solution.py:23
  174.8 1.2 add_select_fusion.6
  176.0 1.2 add_select_fusion.6
  177.3 1.2 add_select_fusion.6
  178.5 1.2 add_select_fusion.6
  181.0 1.2 add_select_fusion.6
  182.2 1.2 add_select_fusion.6
  183.5 1.2 add_select_fusion.6
  184.7 1.2 add_select_fusion.6
  186.0 1.2 add_select_fusion.6
  187.2 1.2 add_select_fusion.6
  188.5 1.2 add_select_fusion.6
  189.7 1.2 add_select_fusion.6
  191.0 1.2 add_select_fusion.6
  192.2 1.2 add_select_fusion.6
  193.5 1.2 add_select_fusion.6
  194.7 1.2 add_select_fusion.6
  196.0 1.2 add_select_fusion.6
  197.2 1.2 add_select_fusion.6
  198.5 1.2 add_select_fusion.6
  199.7 1.2 add_select_fusion.6
  212.8 2.4 multiply_reduce_fusion.4
  216.0 1.8 fusion.48
  218.9 47.2 %all-gather.5 = f32[32,1,512]{2,1,0:T(1,128)S(1)} all-gather(f32[1,1,512]{2,1,0:T(1,128)S(1)} %convolution_bitcast_fusion.3), channel_id=5, replica_groups=mesh['seq'=32,'head'=16] {'seq'}, dimensions={0}, use_global_device_ids=true | all-gather | bytes 67584 | tf_op jit(solution)/shard_map/all_gather | solution.py:11
  266.1 2.1 fusion.5
  268.2 2.9 fusion.7
  271.1 2.1 fusion.4
  273.5 1.9 convolution_bitcast_fusion.2
  275.4 2.8 fusion.49
  278.2 82.3 %all-gather.11.cloned.1.call-done = f32[16384,256]{1,0:T(8,128)} async-done(((f32[512,256]{1,0:T(8,128)}), f32[16384,256]{1,0:T(8,128)}) %all-gather.11.cloned.1.call-update) | async-done | bytes 16777232 | tf_op jit(solution)/shard_map/all_gather | solution.py:11
  360.6 11.6 %rev.6 = f32[32,1,512,256]{3,2,1,0:T(8,128)} reverse(f32[32,1,512,256]{3,2,1,0:T(8,128)} %bitcast.149), dimensions={0} | reverse | bytes 33554432 | tf_op jit(solution)/shard_map/rev | solution.py:13
  372.2 38.7 %while.33 = (s32[]{:T(128)}, f32[1,512,256]{2,1,0:T(8,128)S(1)}, f32[1,512]{1,0:T(1,128)S(1)}, s32[]{:T(128)}, f32[32,1,512,256]{3,2,1,0:T(8,128)}, /*index=5*/f32[32,1,512]{2,1,0:T(1,128)S(1)}, s32[]{:T(128)}, s32[]{:T(128)}) while((s32[]{:T(128)}, f32[1,512,256]{2,1,0:T(8,128)S(1)}, f32[1,512]{1,0:T(1,128)S(1)}, s32[]{:T(128)}, ...), condition=%wide.region_17.18_spmd.clone, body=%wide.region_16.17_spmd.clone.sunk | while | flops 394756 | bytes 1579123 | solution.py:23
  410.8 2.3 fusion.2
  415.1 1.3 dynamic-slice
  417.1 155.2 %all-reduce.3.cloned.1.call-done = f32[256,2,1,256]{3,1,2,0:T(2,128)} async-done(((f32[256,2,1,256]{3,1,2,0:T(2,128)}), f32[256,2,1,256]{3,1,2,0:T(2,128)}) %all-reduce.3.cloned.1.call-update) | async-done | bytes 524304
  (147 shorter events, 63.7 us)
Async XLA Ops:
  7.2 4.4 copy-start
  7.2 166.3 %all-gather.9.cloned.1.call-start = ((), (), s32[]{:S(2)}) async-start(), calls=%async_computation.2 | async-start | bytes 17301504 | tf_op jit(solution)/shard_map/all_gather | solution.py:11
  11.5 206.3 %copy-start.1 = (f32[1,512,256]{1,2,0:T(8,128)}, f32[1,512,256]{1,2,0:T(8,128)S(1)}, u32[]{:S(2)}) copy-start(f32[1,512,256]{1,2,0:T(8,128)S(1)} %get-tuple-element.343) | copy-start | bytes 1572868
  15.3 24.0 %all-to-all-start = ((f32[32,16,256]{2,0,1:T(8,128)}), f32[32,16,256]{2,0,1:T(8,128)S(1)}, u32[]{:S(2)}, u32[]{:S(2)}) async-start(f32[32,16,256]{2,0,1:T(8,128)} %bitcast.151), calls=%async_computation | async-start | bytes 1048576 | tf_op jit(solution)/shard_map/all_to_all | solution.py:39
  41.1 77.8 %all-to-all-start.1 = ((f32[32,16,256]{2,1,0:T(8,128)}), f32[32,16,256]{2,1,0:T(8,128)}, u32[]{:S(2)}, u32[]{:S(2)}) async-start(f32[32,16,256]{2,1,0:T(8,128)} %copy.34), calls=%async_computation.1 | async-start | bytes 1048576 | tf_op jit(solution)/shard_map/all_to_all | solution.py:50
  52.8 307.8 %all-gather.11.cloned.1.call-start = ((), (), s32[]{:S(2)}) async-start(), calls=%async_computation.3 | async-start | bytes 17301504 | tf_op jit(solution)/shard_map/all_gather | solution.py:11
  215.2 0.8 copy-start.3
  217.9 354.4 %all-reduce.3.cloned.1.call-start = ((), (), s32[]{:S(2)}) async-start(), calls=%async_computation.4 | async-start | bytes 1048576
  360.6 52.6 %copy-start.2 = (f32[1,512,256]{1,2,0:T(8,128)S(1)}, f32[1,512,256]{1,2,0:T(8,128)}, u32[]{:S(2)}) copy-start(f32[1,512,256]{1,2,0:T(8,128)} %copy-done.1) | copy-start | bytes 1572868
  360.6 52.8 %copy-start.4 = (f32[512,256]{1,0:T(8,128)S(1)}, f32[512,256]{1,0:T(8,128)}, u32[]{:S(2)}) copy-start(f32[512,256]{1,0:T(8,128)} %param.12) | copy-start | bytes 1572868
Sparse Core Ops, SparseCore 0:
  13.5 159.9 all-gather.8
  218.0 142.5 all-gather.10
  415.3 156.9 all-reduce.2
where the time goes:
time: 585 us; the launch traced here: 581 us
  waiting for transfers between devices  302 us (52%)
  blocking collectives  108 us (18%)
  other arithmetic  78.5 us (13%)
  matrix products  32.3 us (6%)
  local copies, waits for them, and re-layouts  23 us (4%)
  starting transfers between devices  20.8 us (4%)
  between operations  14.6 us (2%)
    unnamed x4, waiting for transfers between devices  155 us
    all_gather x2, waiting for transfers between devices, prefix(): pieces = jax.tree.map(lambda part: lax.all_gather(part, axis), value)  132 us
    all_gather x2, blocking collectives, prefix(): pieces = jax.tree.map(lambda part: lax.all_gather(part, axis), value)  108 us
    select_n x124, other arithmetic, step(): jnp.where(position < mine, new, old)  75.6 us
    all_to_all x1, waiting for transfers between devices, relay_teacher(): lax.all_to_all(teacher_out, 'head', split_axis=1, concat_axis=0, tiled=True)  14.2 us
  transfers between devices with their start and end apart: 5, of which 4 were waited for; matrix products, arithmetic and copies ran while one was open for 5% of the time, Pallas kernels for 0%

commit v1 on v0

v1 whole, which is shorter than its diff:
```python
import jax
import jax.numpy as jnp
from jax import lax
from jax.sharding import PartitionSpec as P

exact_prec = lax.Precision.HIGHEST
work_prec = lax.Precision.HIGH


def dot(spec, a, b, precision=work_prec):
    return jnp.einsum(spec, a, b, precision=precision, preferred_element_type=jnp.float32)


def exchange(value, axis):
    return lax.all_to_all(value, axis, split_axis=0, concat_axis=0, tiled=True)


def ladder_mask(count, backward):
    rows = lax.broadcasted_iota(jnp.int32, (count, count), 0)
    cols = lax.broadcasted_iota(jnp.int32, (count, count), 1)
    keep = cols > rows if backward else cols < rows
    return keep.astype(jnp.float32)


def scan_state(state, backward):
    count = lax.axis_size("seq")
    features, width = state.shape
    pieces = exchange(state.reshape(count, features // count, width), "seq")
    flat = pieces.reshape(count, features // count * width)
    scanned = dot("is,sc->ic", ladder_mask(count, backward), flat, exact_prec)
    back = exchange(scanned.reshape(pieces.shape), "seq")
    return back.reshape(features, width)


def scan_norm(norm, backward):
    count = lax.axis_size("seq")
    mine = lax.axis_index("seq")
    features = norm.shape[0]
    every = jnp.broadcast_to(norm.reshape(1, features // 128, 128), (count, features // 128, 128))
    every = exchange(every, "seq")
    place = lax.broadcasted_iota(jnp.int32, (count, 1, 1), 0)
    keep = place > mine if backward else place < mine
    return jnp.sum(jnp.where(keep, every, 0.0), axis=0).reshape(features)


def back_pair(first_half, second_half, grad_feat, half_feat):
    grad_first = grad_feat[..., :half_feat]
    grad_second = grad_feat[..., half_feat:]
    lead = first_half * (grad_first - jnp.sum(first_half * grad_first, axis=-1, keepdims=True))
    trail = second_half * (grad_second - jnp.sum(second_half * grad_second, axis=-1, keepdims=True))
    return lead - trail


def relay_teacher(teacher_out, block_map):
    gathered = lax.all_to_all(teacher_out, "head", split_axis=1, concat_axis=0, tiled=True)
    seq_count = lax.axis_size("seq")
    position = lax.axis_index("seq")
    columns = gathered.shape[1]
    block_rows = gathered.shape[0] // seq_count
    blocks = gathered.reshape(seq_count, block_rows, columns)
    slot_ids = lax.dynamic_index_in_dim(block_map, position, 0, keepdims=False)
    owner_ids = slot_ids // seq_count
    ladder = jnp.arange(seq_count, dtype=jnp.int32)
    to_owner = (owner_ids[None, :] == ladder[:, None]).astype(jnp.float32)
    by_owner = jnp.einsum("oj,jrc->orc", to_owner, blocks, precision=exact_prec)
    arrived = exchange(by_owner, "seq")
    own_mask = block_map // seq_count == position
    within = jnp.sum(jnp.where(own_mask, block_map % seq_count, 0), axis=1)
    placing = (within[None, :] == ladder[:, None]).astype(jnp.float32)
    placed = jnp.einsum("is,src->irc", placing, arrived, precision=exact_prec)
    return placed.reshape(seq_count * block_rows, columns)


def sum_slices(term):
    count = lax.axis_size("seq")
    rows, width = term.shape
    return jnp.sum(exchange(term.reshape(count, rows // count, width), "seq"), axis=0)


def per_device(queries, keys, values, teacher_out, query_map, key_map, block_map):
    tokens = queries.shape[0]
    half_feat = query_map.shape[2]
    teacher = relay_teacher(teacher_out, block_map)
    pre_k = dot("te,ef->tf", keys, key_map[0], exact_prec)
    first_k = jax.nn.softmax(pre_k, axis=-1)
    second_k = jax.nn.softmax(-pre_k, axis=-1)
    feat_k = jnp.concatenate([first_k, second_k], axis=-1)
    own_state = dot("tf,te->fe", feat_k, values)
    own_norm = jnp.sum(feat_k, axis=0)
    prev_norm = scan_norm(own_norm, False)
    prev_state = scan_state(own_state, False)
    pre_q = dot("te,ef->tf", queries, query_map[0], exact_prec)
    first_q = jax.nn.softmax(pre_q, axis=-1)
    second_q = jax.nn.softmax(-pre_q, axis=-1)
    feat_q = jnp.concatenate([first_q, second_q], axis=-1)
    ladder = jnp.arange(tokens, dtype=jnp.int32)
    causal = ladder[:, None] >= ladder[None, :]
    scores = jnp.where(causal, dot("tf,sf->ts", feat_q, feat_k), 0.0)
    numerator = dot("ts,se->te", scores, values)
    raw_sum = jnp.sum(scores, axis=-1) + jnp.sum(feat_q * prev_norm[None, :], axis=-1)
    numerator = numerator + dot("tf,fe->te", feat_q, prev_state)
    divisor = jnp.maximum(raw_sum, 1.0)
    student = numerator / divisor[:, None]
    mismatch = student - teacher
    grad_num = mismatch / divisor[:, None]
    grad_div = jnp.where(raw_sum > 1.0, -jnp.sum(mismatch * student, axis=-1) / divisor, 0.0)
    own_back = dot("tf,te->fe", feat_q, grad_num)
    own_back_norm = jnp.sum(grad_div[:, None] * feat_q, axis=0)
    next_norm = scan_norm(own_back_norm, True)
    next_state = scan_state(own_back, True)
    weights = jnp.where(causal, dot("te,se->ts", grad_num, values) + grad_div[:, None], 0.0)
    grad_fq = dot("ts,sf->tf", weights, feat_k)
    grad_fq = grad_fq + dot("te,fe->tf", grad_num, prev_state)
    grad_fq = grad_fq + grad_div[:, None] * prev_norm[None, :]
    grad_pq = back_pair(first_q, second_q, grad_fq, half_feat)
    grad_query = sum_slices(dot("te,tf->ef", queries, grad_pq))
    grad_fk = dot("ts,tf->sf", weights, feat_q)
    grad_fk = grad_fk + dot("se,fe->sf", values, next_state)
    grad_fk = grad_fk + next_norm[None, :]
    grad_pk = back_pair(first_k, second_k, grad_fk, half_feat)
    grad_key = sum_slices(dot("te,tf->ef", keys, grad_pk))
    return (grad_query[None], grad_key[None])


def solution(mesh):
    placed = (
        P("seq", "head"),
        P("seq", "head"),
        P("seq", "head"),
        P(("seq", "head"), None),
        P("head", None, None),
        P("head", None, None),
        P(),
    )
    return jax.shard_map(
        per_device,
        mesh=mesh,
        in_specs=placed,
        out_specs=(P("head", "seq", None), P("head", "seq", None)),
        check_vma=False,
    )
```

time: 585 us -> 212 us (0.36)
  the two profiles are of different devices: /device:TPU:16 before, /device:TPU:64 now
where the time goes in v1:
time: 212 us; the launch traced here: 211 us
  waiting for transfers between devices  109 us (51%)
  starting transfers between devices  59.4 us (28%)
  matrix products  28.3 us (13%)
  local copies, waits for them, and re-layouts  9.38 us (4%)
  other arithmetic  3.25 us (2%)
    all_to_all x9, waiting for transfers between devices, exchange(): return lax.all_to_all(value, axis, split_axis=0, concat_axis=0, tiled=True)  94.8 us
    all_to_all x9, starting transfers between devices, exchange(): return lax.all_to_all(value, axis, split_axis=0, concat_axis=0, tiled=True)  52.2 us
    dot_general x16, matrix products, dot(): jnp.einsum(spec, a, b, precision=precision, preferred_element_type=jnp.fl...  25.9 us
    all_to_all x1, waiting for transfers between devices, relay_teacher(): lax.all_to_all(teacher_out, 'head', split_axis=1, concat_axis=0, tiled=True)  14.5 us
    all_to_all x1, starting transfers between devices, relay_teacher(): lax.all_to_all(teacher_out, 'head', split_axis=1, concat_axis=0, tiled=True)  7.21 us
  transfers between devices with their start and end apart: 10, of which 10 were waited for; matrix products, arithmetic and copies ran while one was open for 15% of the time, Pallas kernels for 0%

profile of v1, /device:TPU:64, one launch (start us, length us, event | category | flops | bytes accessed | tf_op | source)
XLA Modules:
  0.0 210.7 jit_solution(18431209424765100003)
XLA Ops:
  0.6 1.8 fusion.73
  3.0 0.6 broadcast_in_dim.44
  3.6 12.6 %all-to-all-start.2 = ((f32[32,4,128]{2,1,0:T(4,128)}), f32[32,4,128]{2,1,0:T(4,128)S(1)}, u32[]{:S(2)}, u32[]{:S(2)}) async-start(f32[32,4,128]{2,1,0:T(4,128)} %broadcast_in_dim.44), calls=%async_computation.2 | async-start | bytes 131072 | tf_op jit(solution)/shard_map/all_to_all | solution.py:15
  16.2 0.8 copy.89
  17.1 8.2 %all-to-all-done.2 = f32[32,4,128]{2,1,0:T(4,128)S(1)} async-done(((f32[32,4,128]{2,1,0:T(4,128)}), f32[32,4,128]{2,1,0:T(4,128)S(1)}, u32[]{:S(2)}, u32[]{:S(2)}) %all-to-all-start.2) | async-done | bytes 65568 | tf_op jit(solution)/shard_map/all_to_all | solution.py:15
  25.3 7.2 %all-to-all-start.3 = ((f32[32,16,256]{2,0,1:T(8,128)}), f32[32,16,256]{2,0,1:T(8,128)S(1)}, u32[]{:S(2)}, u32[]{:S(2)}) async-start(f32[32,16,256]{2,0,1:T(8,128)} %bitcast.94), calls=%async_computation.3 | async-start | bytes 1048576 | tf_op jit(solution)/shard_map/all_to_all | solution.py:55
  32.6 1.4 fusion.31
  34.0 14.5 %all-to-all-done.3 = f32[32,16,256]{2,0,1:T(8,128)S(1)} async-done(((f32[32,16,256]{2,0,1:T(8,128)}), f32[32,16,256]{2,0,1:T(8,128)S(1)}, u32[]{:S(2)}, u32[]{:S(2)}) %all-to-all-start.3) | async-done | bytes 524320 | tf_op jit(solution)/shard_map/all_to_all | solution.py:55
  48.5 4.8 %all-to-all-start = ((f32[32,16,256]{2,1,0:T(8,128)}), f32[32,16,256]{2,1,0:T(8,128)S(1)}, u32[]{:S(2)}, u32[]{:S(2)}) async-start(f32[32,16,256]{2,1,0:T(8,128)} %bitcast.3), calls=%async_computation | async-start | bytes 1048576 | tf_op jit(solution)/shard_map/all_to_all | solution.py:15
  53.5 0.7 fusion.13
  54.2 1.1 copy.54
  55.3 16.2 %all-to-all-done = f32[32,16,256]{2,1,0:T(8,128)S(1)} async-done(((f32[32,16,256]{2,1,0:T(8,128)}), f32[32,16,256]{2,1,0:T(8,128)S(1)}, u32[]{:S(2)}, u32[]{:S(2)}) %all-to-all-start) | async-done | bytes 524320 | tf_op jit(solution)/shard_map/all_to_all | solution.py:15
  71.5 5.4 %all-to-all-start.4 = ((f32[32,16,256]{2,1,0:T(8,128)}), f32[32,16,256]{2,1,0:T(8,128)}, u32[]{:S(2)}, u32[]{:S(2)}) async-start(f32[32,16,256]{2,1,0:T(8,128)} %copy.54), calls=%async_computation.4 | async-start | bytes 1048576 | tf_op jit(solution)/shard_map/all_to_all | solution.py:15
  76.9 0.7 fusion.74
  77.9 2.0 fusion.75
  80.0 0.7 fusion.8
  80.7 1.1 copy.50
  81.8 13.3 %all-to-all-done.4 = f32[32,16,256]{2,1,0:T(8,128)} async-done(((f32[32,16,256]{2,1,0:T(8,128)}), f32[32,16,256]{2,1,0:T(8,128)}, u32[]{:S(2)}, u32[]{:S(2)}) %all-to-all-start.4) | async-done | bytes 524320 | tf_op jit(solution)/shard_map/all_to_all | solution.py:15
  95.1 4.9 %all-to-all-start.1 = ((f32[32,16,256]{2,1,0:T(8,128)}), f32[32,16,256]{2,1,0:T(8,128)}, u32[]{:S(2)}, u32[]{:S(2)}) async-start(f32[32,16,256]{2,1,0:T(8,128)} %copy.50), calls=%async_computation.1 | async-start | bytes 1048576 | tf_op jit(solution)/shard_map/all_to_all | solution.py:15
  100.0 2.7 %fusion.76 = f32[512,256]{0,1:T(8,128)} fusion(f32[512,512]{0,1:T(8,128)} %get-tuple-element.23, f32[512,256]{1,0:T(8,128)S(1)} %copy-done), kind=kOutput, calls=%fused_computation.119 | convolution fusion | flops 402653184 | bytes 2097152 | tf_op jit(solution)/shard_map/ts,se->te/dot_general | solution.py:11
  102.9 1.7 fusion.11
  104.9 1.0 copy.57
  105.9 11.5 %all-to-all-done.1 = f32[32,16,256]{2,1,0:T(8,128)} async-done(((f32[32,16,256]{2,1,0:T(8,128)}), f32[32,16,256]{2,1,0:T(8,128)}, u32[]{:S(2)}, u32[]{:S(2)}) %all-to-all-start.1) | async-done | bytes 524320 | tf_op jit(solution)/shard_map/all_to_all | solution.py:15
  117.4 2.0 multiply_reduce_fusion.6
  119.5 1.4 fusion.48
  120.9 4.9 %all-to-all-start.6 = ((f32[32,16,256]{2,1,0:T(8,128)}), f32[32,16,256]{2,1,0:T(8,128)}, u32[]{:S(2)}, u32[]{:S(2)}) async-start(f32[32,16,256]{2,1,0:T(8,128)} %bitcast.98), calls=%async_computation.6 | async-start | bytes 1048576 | tf_op jit(solution)/shard_map/all_to_all | solution.py:15
  126.0 0.6 fusion.3
  126.7 1.0 copy-done.1
  127.6 2.0 fusion.29
  129.7 13.2 %all-to-all-done.6 = f32[32,16,256]{2,1,0:T(8,128)} async-done(((f32[32,16,256]{2,1,0:T(8,128)}), f32[32,16,256]{2,1,0:T(8,128)}, u32[]{:S(2)}, u32[]{:S(2)}) %all-to-all-start.6) | async-done | bytes 524320 | tf_op jit(solution)/shard_map/all_to_all | solution.py:15
  143.5 4.8 %all-to-all-start.8 = ((f32[32,4,128]{2,1,0:T(4,128)}), f32[32,4,128]{2,1,0:T(4,128)S(1)}, u32[]{:S(2)}, u32[]{:S(2)}) async-start(f32[32,4,128]{2,1,0:T(4,128)} %broadcast_in_dim.81), calls=%async_computation.8 | async-start | bytes 131072 | tf_op jit(solution)/shard_map/all_to_all | solution.py:15
  148.3 1.7 fusion.5
  150.1 1.1 copy.60
  151.2 6.2 %all-to-all-done.8 = f32[32,4,128]{2,1,0:T(4,128)S(1)} async-done(((f32[32,4,128]{2,1,0:T(4,128)}), f32[32,4,128]{2,1,0:T(4,128)S(1)}, u32[]{:S(2)}, u32[]{:S(2)}) %all-to-all-start.8) | async-done | bytes 65568 | tf_op jit(solution)/shard_map/all_to_all | solution.py:15
  157.4 5.4 %all-to-all-start.7 = ((f32[32,16,256]{2,1,0:T(8,128)}), f32[32,16,256]{2,1,0:T(8,128)}, u32[]{:S(2)}, u32[]{:S(2)}) async-start(f32[32,16,256]{2,1,0:T(8,128)} %copy.60), calls=%async_computation.7 | async-start | bytes 1048576 | tf_op jit(solution)/shard_map/all_to_all | solution.py:15
  162.8 2.0 fusion.2
  165.1 0.8 copy-done.4
  165.9 1.3 convolution_bitcast_fusion.2
  167.3 2.0 fusion.49
  169.4 9.2 %all-to-all-done.7 = f32[32,16,256]{2,1,0:T(8,128)} async-done(((f32[32,16,256]{2,1,0:T(8,128)}), f32[32,16,256]{2,1,0:T(8,128)}, u32[]{:S(2)}, u32[]{:S(2)}) %all-to-all-start.7) | async-done | bytes 524320 | tf_op jit(solution)/shard_map/all_to_all | solution.py:15
  178.6 4.9 %all-to-all-start.5 = ((f32[32,8,256]{2,1,0:T(8,128)}), f32[32,8,256]{2,1,0:T(8,128)S(1)}, u32[]{:S(2)}, u32[]{:S(2)}) async-start(f32[32,8,256]{2,1,0:T(8,128)} %convolution_bitcast_fusion.2), calls=%async_computation.5 | async-start | bytes 524288 | tf_op jit(solution)/shard_map/all_to_all | solution.py:15
  183.5 2.0 fusion.1
  185.8 0.8 copy-done.5
  186.6 1.3 convolution_bitcast_fusion.1
  187.9 6.6 %all-to-all-done.5 = f32[32,8,256]{2,1,0:T(8,128)S(1)} async-done(((f32[32,8,256]{2,1,0:T(8,128)}), f32[32,8,256]{2,1,0:T(8,128)S(1)}, u32[]{:S(2)}, u32[]{:S(2)}) %all-to-all-start.5) | async-done | bytes 262176 | tf_op jit(solution)/shard_map/all_to_all | solution.py:15
  194.5 4.5 %all-to-all-start.9 = ((f32[32,8,256]{2,1,0:T(8,128)}), f32[32,8,256]{2,1,0:T(8,128)S(1)}, u32[]{:S(2)}, u32[]{:S(2)}) async-start(f32[32,8,256]{2,1,0:T(8,128)} %convolution_bitcast_fusion.1), calls=%async_computation.9 | async-start | bytes 524288 | tf_op jit(solution)/shard_map/all_to_all | solution.py:15
  199.0 0.6 reduce_sum.174
  199.6 10.4 %all-to-all-done.9 = f32[32,8,256]{2,1,0:T(8,128)S(1)} async-done(((f32[32,8,256]{2,1,0:T(8,128)}), f32[32,8,256]{2,1,0:T(8,128)S(1)}, u32[]{:S(2)}, u32[]{:S(2)}) %all-to-all-start.9) | async-done | bytes 262176 | tf_op jit(solution)/shard_map/all_to_all | solution.py:15
  (35 shorter events, 3.6 us)
Async XLA Ops:
  0.6 31.9 %copy-start = (f32[512,256]{1,0:T(8,128)S(1)}, f32[512,256]{1,0:T(8,128)}, u32[]{:S(2)}) copy-start(f32[512,256]{1,0:T(8,128)} %param.9) | copy-start | bytes 1572868
  2.8 13.4 %copy-start.6 = (f32[32,4096]{1,0:T(8,128)S(1)}, f32[32,4096]{1,0:T(8,128)}, u32[]{:S(2)}) copy-start(f32[32,4096]{1,0:T(8,128)} %param.10) | copy-start | bytes 1572868
  3.6 21.7 %all-to-all-start.2 = ((f32[32,4,128]{2,1,0:T(4,128)}), f32[32,4,128]{2,1,0:T(4,128)S(1)}, u32[]{:S(2)}, u32[]{:S(2)}) async-start(f32[32,4,128]{2,1,0:T(4,128)} %broadcast_in_dim.44), calls=%async_computation.2 | async-start | bytes 131072 | tf_op jit(solution)/shard_map/all_to_all | solution.py:15
  25.3 23.2 %all-to-all-start.3 = ((f32[32,16,256]{2,0,1:T(8,128)}), f32[32,16,256]{2,0,1:T(8,128)S(1)}, u32[]{:S(2)}, u32[]{:S(2)}) async-start(f32[32,16,256]{2,0,1:T(8,128)} %bitcast.94), calls=%async_computation.3 | async-start | bytes 1048576 | tf_op jit(solution)/shard_map/all_to_all | solution.py:55
  48.5 4.8 %copy-start.8 = (s32[32,32]{1,0:T(8,128)S(1)}, s32[32,32]{1,0:T(8,128)}, u32[]{:S(2)}) copy-start(s32[32,32]{1,0:T(8,128)} %param.13) | copy-start | bytes 12292
  48.5 23.0 %all-to-all-start = ((f32[32,16,256]{2,1,0:T(8,128)}), f32[32,16,256]{2,1,0:T(8,128)S(1)}, u32[]{:S(2)}, u32[]{:S(2)}) async-start(f32[32,16,256]{2,1,0:T(8,128)} %bitcast.3), calls=%async_computation | async-start | bytes 1048576 | tf_op jit(solution)/shard_map/all_to_all | solution.py:15
  55.3 21.6 %copy-start.3 = (f32[512,256]{1,0:T(8,128)S(1)}, f32[512,256]{1,0:T(8,128)}, u32[]{:S(2)}) copy-start(f32[512,256]{1,0:T(8,128)} %param.7) | copy-start | bytes 1572868
  55.3 21.6 %copy-start.7 = (f32[1,256,256]{2,1,0:T(8,128)S(1)}, f32[1,256,256]{2,1,0:T(8,128)}, u32[]{:S(2)}) copy-start(f32[1,256,256]{2,1,0:T(8,128)} %param.11) | copy-start | bytes 786436
  71.5 23.6 %all-to-all-start.4 = ((f32[32,16,256]{2,1,0:T(8,128)}), f32[32,16,256]{2,1,0:T(8,128)}, u32[]{:S(2)}, u32[]{:S(2)}) async-start(f32[32,16,256]{2,1,0:T(8,128)} %copy.54), calls=%async_computation.4 | async-start | bytes 1048576 | tf_op jit(solution)/shard_map/all_to_all | solution.py:15
  95.1 22.4 %all-to-all-start.1 = ((f32[32,16,256]{2,1,0:T(8,128)}), f32[32,16,256]{2,1,0:T(8,128)}, u32[]{:S(2)}, u32[]{:S(2)}) async-start(f32[32,16,256]{2,1,0:T(8,128)} %copy.50), calls=%async_computation.1 | async-start | bytes 1048576 | tf_op jit(solution)/shard_map/all_to_all | solution.py:15
  120.9 21.9 %all-to-all-start.6 = ((f32[32,16,256]{2,1,0:T(8,128)}), f32[32,16,256]{2,1,0:T(8,128)}, u32[]{:S(2)}, u32[]{:S(2)}) async-start(f32[32,16,256]{2,1,0:T(8,128)} %bitcast.98), calls=%async_computation.6 | async-start | bytes 1048576 | tf_op jit(solution)/shard_map/all_to_all | solution.py:15
  126.7 1.0 copy-start.1
  143.5 14.0 %all-to-all-start.8 = ((f32[32,4,128]{2,1,0:T(4,128)}), f32[32,4,128]{2,1,0:T(4,128)S(1)}, u32[]{:S(2)}, u32[]{:S(2)}) async-start(f32[32,4,128]{2,1,0:T(4,128)} %broadcast_in_dim.81), calls=%async_computation.8 | async-start | bytes 131072 | tf_op jit(solution)/shard_map/all_to_all | solution.py:15
  157.4 21.2 %all-to-all-start.7 = ((f32[32,16,256]{2,1,0:T(8,128)}), f32[32,16,256]{2,1,0:T(8,128)}, u32[]{:S(2)}, u32[]{:S(2)}) async-start(f32[32,16,256]{2,1,0:T(8,128)} %copy.60), calls=%async_computation.7 | async-start | bytes 1048576 | tf_op jit(solution)/shard_map/all_to_all | solution.py:15
  164.9 1.0 copy-start.4
  165.9 1.3 copy-start.2
  178.6 15.9 %all-to-all-start.5 = ((f32[32,8,256]{2,1,0:T(8,128)}), f32[32,8,256]{2,1,0:T(8,128)S(1)}, u32[]{:S(2)}, u32[]{:S(2)}) async-start(f32[32,8,256]{2,1,0:T(8,128)} %convolution_bitcast_fusion.2), calls=%async_computation.5 | async-start | bytes 524288 | tf_op jit(solution)/shard_map/all_to_all | solution.py:15
  185.5 1.0 copy-start.5
  194.5 15.5 %all-to-all-start.9 = ((f32[32,8,256]{2,1,0:T(8,128)}), f32[32,8,256]{2,1,0:T(8,128)S(1)}, u32[]{:S(2)}, u32[]{:S(2)}) async-start(f32[32,8,256]{2,1,0:T(8,128)} %convolution_bitcast_fusion.1), calls=%async_computation.9 | async-start | bytes 524288 | tf_op jit(solution)/shard_map/all_to_all | solution.py:15

commit v2 on v1

v2 whole, which is shorter than its diff:
```python
import functools

import jax
import jax.numpy as jnp
from jax import lax
from jax.experimental import pallas as pl
from jax.experimental.pallas import tpu as pltpu
from jax.sharding import PartitionSpec as P

exact_prec = lax.Precision.HIGHEST
LANES = 128
CORES = 2
HEAD_WIDTH = 256
ROWS = 8
NN = (((1,), (0,)), ((), ()))
NT = (((1,), (1,)), ((), ()))
TN = (((0,), (0,)), ((), ()))


def halves(x):
    high = x.astype(jnp.bfloat16)
    return high, (x - high.astype(jnp.float32)).astype(jnp.bfloat16)


def dot3(a, b, dims):
    def one(x, y):
        return lax.dot_general(x, y, dims, preferred_element_type=jnp.float32)

    return one(a[0], b[0]) + (one(a[0], b[1]) + one(a[1], b[0]))


def features(rows, weights):
    pre = lax.dot_general(rows, weights, NN, precision=exact_prec, preferred_element_type=jnp.float32)
    first = jnp.exp(pre - jnp.max(pre, axis=-1, keepdims=True))
    second = jnp.exp(jnp.min(pre, axis=-1, keepdims=True) - pre)
    first = first / jnp.sum(first, axis=-1, keepdims=True)
    second = second / jnp.sum(second, axis=-1, keepdims=True)
    return first, second


def pack(out_ref, base, value):
    owners = out_ref.shape[0]
    for c in range(value.shape[1] // LANES):
        part = value[:, c * LANES : (c + 1) * LANES]
        out_ref[:, base + c * ROWS : base + (c + 1) * ROWS, :] = part.reshape(owners, ROWS, LANES)


def unpack(ref, base, count):
    owners = ref.shape[0]
    parts = [
        ref[:, base + c * ROWS : base + (c + 1) * ROWS, :].reshape(owners * ROWS, LANES)
        for c in range(count)
    ]
    return jnp.concatenate(parts, axis=-1)


def pack_norm(out_ref, base, norm):
    owners = out_ref.shape[0]
    count = norm.shape[1] // LANES
    rows = [norm[:, c * LANES : (c + 1) * LANES] for c in range(count)]
    rows.append(jnp.zeros((ROWS - count, LANES), jnp.float32))
    tile = jnp.concatenate(rows, axis=0)
    out_ref[:, base : base + ROWS, :] = jnp.broadcast_to(tile[None], (owners, ROWS, LANES))


def key_kernel(keys, weights, values, feat_ref, out_ref):
    half = weights.shape[1]
    first, second = features(keys[...], weights[...])
    feat_ref[:, :half] = first
    feat_ref[:, half:] = second
    feat = feat_ref[...]
    state = dot3(halves(values[...]), halves(feat), TN)
    width = state.shape[1] // LANES
    pack(out_ref, 0, state)
    pack_norm(out_ref, width * ROWS, jnp.sum(feat, axis=0, keepdims=True))


def query_kernel(queries, weights, feat_k, values, feat_ref, numer_ref, raw_ref):
    half = weights.shape[1]
    tokens = queries.shape[0]
    step = 256
    first, second = features(queries[...], weights[...])
    feat_ref[:, :half] = first
    feat_ref[:, half:] = second
    vals = halves(values[...])
    keys = halves(feat_k[...])
    for lo in range(0, tokens, step):
        hi = lo + step
        fq = halves(feat_ref[lo:hi, :])
        scores = dot3(fq, (keys[0][:hi], keys[1][:hi]), NT)
        t = lax.broadcasted_iota(jnp.int32, scores.shape, 0) + lo
        s = lax.broadcasted_iota(jnp.int32, scores.shape, 1)
        scores = jnp.where(t >= s, scores, 0.0)
        raw_ref[lo:hi, :] = jnp.sum(scores, axis=-1, keepdims=True)
        numer_ref[lo:hi, :] = dot3(halves(scores), (vals[0][:hi], vals[1][:hi]), NN)


def scan_kernel(backward, state_rows, mine_ref, got_ref, out_ref, norm_ref):
    count = got_ref.shape[0]
    mine = mine_ref[0]
    total = jnp.zeros((state_rows, LANES), jnp.float32)
    norm = jnp.zeros((ROWS, LANES), jnp.float32)
    for place in range(count - 1, -1, -1) if backward else range(count):
        out_ref[place, :state_rows, :] = total
        total = total + got_ref[place, :state_rows, :]
        use = (place > mine) if backward else (place < mine)
        tile = got_ref[place, state_rows : state_rows + ROWS, :]
        norm = norm + jnp.where(use, tile, 0.0)
    norm_ref[...] = norm


def partner_kernel(place_ref, teacher_ref, out_ref):
    other = 1 - place_ref[1] % CORES
    width = teacher_ref.shape[1] // place_count(teacher_ref)
    for pair in range(place_count(teacher_ref) // CORES):
        at = pl.multiple_of((pair * CORES + other) * width, width)
        out_ref[:, pair * width : (pair + 1) * width] = teacher_ref[:, pl.ds(at, width)]


def place_count(teacher_ref):
    return teacher_ref.shape[1] // HEAD_WIDTH


def spread_kernel(place_ref, teacher_ref, got_ref, *out_refs):
    core = place_ref[1] % CORES
    chip = place_ref[1] // CORES
    rows = teacher_ref.shape[0]
    ring = len(out_refs)
    mine = pl.multiple_of(core * rows, rows)
    theirs = pl.multiple_of((1 - core) * rows, rows)
    for k, out_ref in enumerate(out_refs):
        to = (chip + k) % ring
        at = pl.multiple_of((to * CORES + core) * HEAD_WIDTH, HEAD_WIDTH)
        out_ref[pl.ds(mine, rows), :] = teacher_ref[:, pl.ds(at, HEAD_WIDTH)]
        at = pl.multiple_of(to * HEAD_WIDTH, HEAD_WIDTH)
        out_ref[pl.ds(theirs, rows), :] = got_ref[:, pl.ds(at, HEAD_WIDTH)]


def forward_scan_kernel(state_rows, rows, place_ref, owner_ref, got_ref, *refs):
    blocks_refs, (out_ref, norm_ref) = refs[:-2], refs[-2:]
    scan_kernel(False, state_rows, place_ref, got_ref, out_ref, norm_ref)
    ring = len(blocks_refs)
    chip = place_ref[1] // CORES
    for k, blocks_ref in enumerate(blocks_refs):
        source = (chip + ring - k) % ring
        each = blocks_ref.shape[0] // rows
        for m in range(each):
            owner = owner_ref[source * each + m]
            for c in range(HEAD_WIDTH // LANES):
                base = state_rows + c * rows
                out_ref[owner, base : base + rows, :] = blocks_ref[
                    m * rows : (m + 1) * rows, c * LANES : (c + 1) * LANES
                ]


def backward_scan_kernel(state_rows, mine_ref, got_ref, term_ref, out_ref, norm_ref):
    scan_kernel(True, state_rows, mine_ref, got_ref, out_ref, norm_ref)
    out_ref[:, state_rows:, :] = term_ref[...]


def norm_row(norm_ref, count):
    return jnp.concatenate([norm_ref[c : c + 1, :] for c in range(count)], axis=-1)


def middle_kernel(
    block_rows, within_ref, got_ref, norm_ref, feat_q, numer, raw,
    state_ref, grad_ref, div_ref, out_ref, teacher_ref,
):
    feats = feat_q.shape[1]
    width = numer.shape[1]
    count = got_ref.shape[0]
    chunks = feats // LANES
    state_rows = chunks * ROWS
    state = unpack(got_ref, 0, chunks)
    state_ref[...] = state
    for source in range(count):
        at = pl.multiple_of(within_ref[source] * block_rows, block_rows)
        for c in range(width // LANES):
            base = state_rows + c * block_rows
            teacher_ref[pl.ds(at, block_rows), c * LANES : (c + 1) * LANES] = got_ref[
                source, base : base + block_rows, :
            ]
    fq = feat_q[...]
    fq_pair = halves(fq)
    numerator = numer[...] + dot3(fq_pair, halves(state), NT)
    prev_norm = norm_row(norm_ref, chunks)
    raw_sum = raw[...] + jnp.sum(fq * prev_norm, axis=-1, keepdims=True)
    divisor = jnp.maximum(raw_sum, 1.0)
    student = numerator / divisor
    mismatch = student - teacher_ref[...]
    grad_num = mismatch / divisor
    grad_div = jnp.where(raw_sum > 1.0, -jnp.sum(mismatch * student, axis=-1, keepdims=True) / divisor, 0.0)
    grad_ref[...] = grad_num
    div_ref[...] = grad_div
    pack(out_ref, 0, dot3(halves(grad_num), fq_pair, TN))
    pack_norm(out_ref, state_rows, jnp.sum(grad_div * fq, axis=0, keepdims=True))


def back_pair(feat, grad, half):
    first, second = feat[:, :half], feat[:, half:]
    grad_first, grad_second = grad[:, :half], grad[:, half:]
    lead = first * (grad_first - jnp.sum(first * grad_first, axis=-1, keepdims=True))
    trail = second * (grad_second - jnp.sum(second * grad_second, axis=-1, keepdims=True))
    return lead - trail


def weight_kernel(
    queries, values, feat_q, feat_k, state, norm_ref, grad_num, grad_div, term_ref, inner_ref, pre_ref
):
    tokens, feats = feat_q.shape
    half = feats // 2
    step = 256
    chunks = feats // LANES
    vals = halves(values[...])
    keys = halves(feat_k[...])
    states = halves(state[...])
    prev_norm = norm_row(norm_ref, chunks)
    for lo in range(0, tokens, step):
        hi = lo + step
        div = grad_div[lo:hi, :]
        num = halves(grad_num[lo:hi, :])
        fq = feat_q[lo:hi, :]
        weights = dot3(num, (vals[0][:hi], vals[1][:hi]), NT) + div
        t = lax.broadcasted_iota(jnp.int32, weights.shape, 0) + lo
        s = lax.broadcasted_iota(jnp.int32, weights.shape, 1)
        weights = halves(jnp.where(t >= s, weights, 0.0))
        grad_fq = dot3(weights, (keys[0][:hi], keys[1][:hi]), NN) + dot3(num, states, NN) + div * prev_norm
        pre_ref[lo:hi, :] = back_pair(fq, grad_fq, half)
        part = dot3(weights, halves(fq), TN)
        if lo == 0:
            inner_ref[:hi, :] = part
        else:
            inner_ref[:lo, :] = inner_ref[:lo, :] + part[:lo]
            inner_ref[lo:hi, :] = part[lo:]
    pack(term_ref, 0, dot3(halves(queries[...]), halves(pre_ref[...]), TN))


def close_kernel(keys, values, feat_k, inner, got_ref, norm_ref, term_ref, query_ref):
    feats = feat_k.shape[1]
    chunks = feats // LANES
    state = unpack(got_ref, 0, chunks)
    grad_fk = inner[...] + dot3(halves(values[...]), halves(state), NN) + norm_row(norm_ref, chunks)
    grad_pk = back_pair(feat_k[...], grad_fk, feats // 2)
    pack(term_ref, 0, dot3(halves(keys[...]), halves(grad_pk), TN))
    sum_kernel(chunks * ROWS, got_ref, query_ref)


def sum_kernel(base, got_ref, out_ref):
    for c in range(out_ref.shape[1] // LANES):
        part = got_ref[:, base + c * ROWS : base + (c + 1) * ROWS, :]
        out_ref[:, c * LANES : (c + 1) * LANES] = jnp.sum(part, axis=0)


def call(body, outs, spaces, cost, args, scratch=()):
    vmem = pl.BlockSpec(memory_space=pltpu.VMEM)
    smem = pl.BlockSpec(memory_space=pltpu.SMEM)
    return pl.pallas_call(
        body,
        out_shape=[jax.ShapeDtypeStruct(shape, jnp.float32) for shape in outs],
        in_specs=[smem if kind == "s" else vmem for kind in spaces],
        out_specs=[vmem] * len(outs),
        scratch_shapes=[pltpu.VMEM(shape, jnp.float32) for shape in scratch],
        compiler_params=pltpu.CompilerParams(vmem_limit_bytes=24 * 1024 * 1024),
        cost_estimate=pl.CostEstimate(flops=int(cost * 1e9), bytes_accessed=1 << 20, transcendentals=0),
    )(*args)


def exchange(value, axis):
    return lax.all_to_all(value, axis, split_axis=0, concat_axis=0, tiled=True)


def per_device(queries, keys, values, teacher_out, query_map, key_map, block_map):
    tokens, width = queries.shape
    half = query_map.shape[2]
    feats = 2 * half
    count = lax.axis_size("seq")
    mine = lax.axis_index("seq")
    heads = lax.axis_size("head")
    chunks = feats // LANES
    state_rows = chunks * ROWS
    block_rows = tokens // count
    term_rows = half // LANES * ROWS

    place = jnp.stack([mine, lax.axis_index("head")]).astype(jnp.int32)
    slot_ids = lax.dynamic_index_in_dim(block_map, mine, 0, keepdims=False)
    owner_ids = slot_ids // count
    within = jnp.sum(jnp.where(block_map // count == mine, block_map % count, 0), axis=1).astype(jnp.int32)
    ring = heads // CORES
    rows = teacher_out.shape[0]
    (partner,) = call(partner_kernel, [(rows, ring * width)], "sv", 0.1, (place, teacher_out))
    partner = lax.ppermute(partner, "head", [(h, h ^ 1) for h in range(heads)])
    feat_k, out1 = call(
        key_kernel, [(tokens, feats), (count, state_rows + ROWS, LANES)], "vvv", 1.0,
        (keys, key_map[0], values),
    )
    got1 = exchange(out1, "seq")
    blocks = call(spread_kernel, [(CORES * rows, width)] * ring, "svv", 0.1, (place, teacher_out, partner))
    blocks = list(blocks[:1]) + [
        lax.ppermute(blocks[k], "head", [(h, (h + CORES * k) % heads) for h in range(heads)])
        for k in range(1, ring)
    ]
    feat_q, numer, raw = call(
        query_kernel, [(tokens, feats), (tokens, width), (tokens, 1)], "vvvv", 2.0,
        (queries, query_map[0], feat_k, values),
    )
    out2, prev_norm = call(
        functools.partial(forward_scan_kernel, state_rows, block_rows),
        [(count, state_rows + block_rows * (width // LANES), LANES), (ROWS, LANES)],
        "ssv" + "v" * ring, 0.1, (place, owner_ids, got1, *blocks),
    )
    got2 = exchange(out2, "seq")
    state, grad_num, grad_div, out3 = call(
        functools.partial(middle_kernel, block_rows),
        [(width, feats), (tokens, width), (tokens, 1), (count, state_rows + ROWS, LANES)],
        "svvvvv", 1.0, (within, got2, prev_norm, feat_q, numer, raw), [(tokens, width)],
    )
    got3 = exchange(out3, "seq")
    term_q, inner = call(
        weight_kernel, [(count, term_rows, LANES), (tokens, feats)], "vvvvvvvv", 4.0,
        (queries, values, feat_q, feat_k, state, prev_norm, grad_num, grad_div), [(tokens, half)],
    )
    out4, next_norm = call(
        functools.partial(backward_scan_kernel, state_rows),
        [(count, state_rows + term_rows, LANES), (ROWS, LANES)],
        "svv", 0.1, (place, got3, term_q),
    )
    got4 = exchange(out4, "seq")
    out5, grad_query = call(
        close_kernel, [(count, term_rows, LANES), (width // count, half)], "vvvvvv", 1.0,
        (keys, values, feat_k, inner, got4, next_norm),
    )
    got5 = exchange(out5, "seq")
    (grad_key,) = call(functools.partial(sum_kernel, 0), [(width // count, half)], "v", 0.1, (got5,))
    return (grad_query[None], grad_key[None])


def solution(mesh):
    placed = (
        P("seq", "head"),
        P("seq", "head"),
        P("seq", "head"),
        P(("seq", "head"), None),
        P("head", None, None),
        P("head", None, None),
        P(),
    )
    return jax.shard_map(
        per_device,
        mesh=mesh,
        in_specs=placed,
        out_specs=(P("head", "seq", None), P("head", "seq", None)),
        check_vma=False,
    )
```

time: 212 us -> 176 us (0.83)
  the two profiles are of different devices: /device:TPU:64 before, /device:TPU:24 now
where the time goes in v2:
time: 176 us; the launch traced here: 174 us
  starting transfers between devices  56.5 us (32%)
  blocking collectives  43.1 us (24%)
  waiting for transfers between devices  40 us (23%)
  Pallas kernels  18.5 us (11%)
  local copies, waits for them, and re-layouts  15.1 us (9%)
    all_to_all x2, blocking collectives, exchange(): return lax.all_to_all(value, axis, split_axis=0, concat_axis=0, tiled=True)  43.1 us
    all_to_all x3, waiting for transfers between devices, exchange(): return lax.all_to_all(value, axis, split_axis=0, concat_axis=0, tiled=True)  34.2 us
    all_to_all x3, starting transfers between devices, exchange(): return lax.all_to_all(value, axis, split_axis=0, concat_axis=0, tiled=True)  28.2 us
    ppermute x7, starting transfers between devices, per_device(): lax.ppermute(blocks[k], 'head', [(h, (h + CORES * k) % heads) for h in ra...  26.5 us
    pallas_call x10, Pallas kernels, call(): pl.pallas_call(body, out_shape=[jax.ShapeDtypeStruct(shape, jnp.float32)...  18.5 us
    unnamed x48, local copies, waits for them, and re-layouts  15.1 us
    ppermute x7, waiting for transfers between devices, per_device(): lax.ppermute(blocks[k], 'head', [(h, (h + CORES * k) % heads) for h in ra...  4.32 us
  transfers between devices with their start and end apart: 11, of which 6 were waited for; matrix products, arithmetic and copies ran while one was open for 0% of the time, Pallas kernels for 4%

profile of v2, /device:TPU:24, one launch (start us, length us, event | category | flops | bytes accessed | tf_op | source)
XLA Modules:
  0.0 174.4 jit_solution(9307480345924621279)
XLA Ops:
  0.6 1.0 copy-done.1
  1.7 1.0 copy-done.3
  2.7 0.9 copy-done.8
  3.7 3.0 %shard_map.86 = (f32[512,512]{1,0:T(8,128)S(1)}, f32[32,40,128]{2,1,0:T(8,128)}) custom-call(f32[512,256]{1,0:T(8,128)S(1)} %copy-done.1, f32[256,256]{1,0:T(8,128)S(1)} %bitcast.14, f32[512,256]{1,0:T(8,128)S(1)} %copy-done.3), custom_call_target="tpu_custom_call" | custom-call | flops 1000000000 | bytes 1048576 | tf_op jit(solution)/shard_map/pallas_call | solution.py:257
  6.7 13.3 %all-to-all-start = ((f32[32,40,128]{2,1,0:T(8,128)}), f32[32,40,128]{2,1,0:T(8,128)S(1)}, u32[]{:S(2)}, u32[]{:S(2)}) async-start(f32[32,40,128]{2,1,0:T(8,128)} %get-tuple-element.29), calls=%async_computation | async-start | bytes 1310720 | tf_op jit(solution)/shard_map/all_to_all | solution.py:269
  20.0 0.1 pad_add_fusion.place_ref.mine_ref
  20.1 0.6 shard_map.88
  20.6 1.9 %collective-permute-start = (f32[32,2048]{1,0:T(8,128)S(1)}, f32[32,2048]{1,0:T(8,128)S(1)}, u32[]{:S(2)}, u32[]{:S(2)}) collective-permute-start(f32[32,2048]{1,0:T(8,128)S(1)} %shard_map.88), channel_id=1, source_target_pairs={{0,1},{1,0},{2,3},{3,2},{4,5},{5,4},{6,7},{7,6},{8,9},{9,8},{10,11... | collective-permute-start | bytes 786440 | tf_op jit(solution)/shard_map/ppermute | solution.py:291
  22.6 1.5 collective-permute-done.got_ref
  24.1 0.6 shard_map.89
  24.7 4.7 %collective-permute-start.1 = (f32[64,256]{1,0:T(8,128)S(1)}, f32[64,256]{1,0:T(8,128)S(1)}, u32[]{:S(2)}, u32[]{:S(2)}) collective-permute-start(f32[64,256]{1,0:T(8,128)S(1)} %get-tuple-element.31), channel_id=1, source_target_pairs={{0,2},{1,3},{2,4},{3,5},{4,6},{5,7},{6,8},{7,9},{8,10},{9,11},{10,... | collective-permute-start | bytes 196616 | tf_op jit(solution)/shard_map/ppermute | solution.py:299
  29.4 2.7 %collective-permute-start.2 = (f32[64,256]{1,0:T(8,128)S(1)}, f32[64,256]{1,0:T(8,128)S(1)}, u32[]{:S(2)}, u32[]{:S(2)}) collective-permute-start(f32[64,256]{1,0:T(8,128)S(1)} %get-tuple-element.32), channel_id=1, source_target_pairs={{0,4},{1,5},{2,6},{3,7},{4,8},{5,9},{6,10},{7,11},{8,12},{9,13},{1... | collective-permute-start | bytes 196616 | tf_op jit(solution)/shard_map/ppermute | solution.py:299
  32.1 2.8 %collective-permute-start.3 = (f32[64,256]{1,0:T(8,128)S(1)}, f32[64,256]{1,0:T(8,128)S(1)}, u32[]{:S(2)}, u32[]{:S(2)}) collective-permute-start(f32[64,256]{1,0:T(8,128)S(1)} %get-tuple-element.33), channel_id=1, source_target_pairs={{0,6},{1,7},{2,8},{3,9},{4,10},{5,11},{6,12},{7,13},{8,14},{9,15},... | collective-permute-start | bytes 196616 | tf_op jit(solution)/shard_map/ppermute | solution.py:299
  34.9 6.8 %collective-permute-start.4 = (f32[64,256]{1,0:T(8,128)S(1)}, f32[64,256]{1,0:T(8,128)S(1)}, u32[]{:S(2)}, u32[]{:S(2)}) collective-permute-start(f32[64,256]{1,0:T(8,128)S(1)} %get-tuple-element.34), channel_id=1, source_target_pairs={{0,8},{1,9},{2,10},{3,11},{4,12},{5,13},{6,14},{7,15},{8,0},{9,1},... | collective-permute-start | bytes 196616 | tf_op jit(solution)/shard_map/ppermute | solution.py:299
  41.8 1.9 %collective-permute-start.5 = (f32[64,256]{1,0:T(8,128)S(1)}, f32[64,256]{1,0:T(8,128)S(1)}, u32[]{:S(2)}, u32[]{:S(2)}) collective-permute-start(f32[64,256]{1,0:T(8,128)S(1)} %get-tuple-element.35), channel_id=1, source_target_pairs={{0,10},{1,11},{2,12},{3,13},{4,14},{5,15},{6,0},{7,1},{8,2},{9,3},... | collective-permute-start | bytes 196616 | tf_op jit(solution)/shard_map/ppermute | solution.py:299
  43.7 3.6 %collective-permute-start.6 = (f32[64,256]{1,0:T(8,128)S(1)}, f32[64,256]{1,0:T(8,128)S(1)}, u32[]{:S(2)}, u32[]{:S(2)}) collective-permute-start(f32[64,256]{1,0:T(8,128)S(1)} %get-tuple-element.36), channel_id=1, source_target_pairs={{0,12},{1,13},{2,14},{3,15},{4,0},{5,1},{6,2},{7,3},{8,4},{9,5},{1... | collective-permute-start | bytes 196616 | tf_op jit(solution)/shard_map/ppermute | solution.py:299
  47.3 3.9 %collective-permute-start.7 = (f32[64,256]{1,0:T(8,128)S(1)}, f32[64,256]{1,0:T(8,128)S(1)}, u32[]{:S(2)}, u32[]{:S(2)}) collective-permute-start(f32[64,256]{1,0:T(8,128)S(1)} %get-tuple-element.37), channel_id=1, source_target_pairs={{0,14},{1,15},{2,0},{3,1},{4,2},{5,3},{6,4},{7,5},{8,6},{9,7},{10,... | collective-permute-start | bytes 196616 | tf_op jit(solution)/shard_map/ppermute | solution.py:299
  51.3 2.5 %collective-permute-done.5.refs_5_ = f32[64,256]{1,0:T(8,128)S(1)} collective-permute-done((f32[64,256]{1,0:T(8,128)S(1)}, f32[64,256]{1,0:T(8,128)S(1)}, u32[]{:S(2)}, u32[]{:S(2)}) %collective-permute-start.5) | collective-permute-done | bytes 65568 | tf_op jit(solution)/shard_map/ppermute | solution.py:299
  53.8 1.7 collective-permute-done.6.refs_6_
  55.5 0.1 collective-permute-done.7.refs_7_
  55.6 1.6 shard_map.90
  57.2 9.9 %all-to-all-start.1 = ((f32[32,64,128]{2,1,0:T(8,128)}), f32[32,64,128]{2,1,0:T(8,128)S(1)}, u32[]{:S(2)}, u32[]{:S(2)}) async-start(f32[32,64,128]{2,1,0:T(8,128)} %get-tuple-element.38), calls=%async_computation.1 | async-start | bytes 2097152 | tf_op jit(solution)/shard_map/all_to_all | solution.py:269
  67.2 0.1 fusion.2.within_ref
  67.3 3.0 %shard_map.87 = (f32[512,512]{1,0:T(8,128)S(1)}, f32[512,256]{1,0:T(8,128)S(1)}, f32[512,1]{1,0:T(8,128)S(1)}) custom-call(f32[512,256]{1,0:T(8,128)S(1)} %copy-done.6, f32[256,256]{1,0:T(8,128)S(1)} %bitcast.15, f32[512,512]{1,0:T(8,128)S(1)} %get-tuple-element.27.feat_k, f32[512,256]{1,0:T(8,128)S(1)} %copy-done.4), custom_call_target="tpu_custom_call" | custom-call | flops 2000000000 | bytes 1048576 | tf_op jit(solution)/shard_map/pallas_call | solution.py:257
  70.3 1.0 copy-done.10
  71.3 0.8 copy-done.17
  72.1 0.7 copy-done.21
  72.8 22.6 %all-to-all-done.1.got_ref = f32[32,64,128]{2,1,0:T(8,128)S(1)} async-done(((f32[32,64,128]{2,1,0:T(8,128)}), f32[32,64,128]{2,1,0:T(8,128)S(1)}, u32[]{:S(2)}, u32[]{:S(2)}) %all-to-all-start.1) | async-done | bytes 1048608 | tf_op jit(solution)/shard_map/all_to_all | solution.py:269
  95.5 1.2 copy-done.11
  96.7 1.0 copy-done.18
  97.7 0.9 copy-done.22
  98.7 3.4 %shard_map.91 = (f32[256,512]{1,0:T(8,128)S(1)}, f32[512,256]{1,0:T(8,128)S(1)}, f32[512,1]{1,0:T(8,128)S(1)}, f32[32,40,128]{2,1,0:T(8,128)}) custom-call(s32[32]{0:T(128)S(1)} %fusion.2.within_ref, f32[32,64,128]{2,1,0:T(8,128)S(1)} %all-to-all-done.1.got_ref, f32[8,128]{1,0:T(8,128)S(1)} %get-tuple-element.39.norm_ref, f32[512,512]{1,0:T(8,128)S(1)} %copy-done.11, ...), custom_call_target="tpu_custom_call" | custom-call | flops 1000000000 | bytes 1048576 | tf_op jit(solution)/shard_map/pallas_call | solution.py:257
  102.1 0.8 copy-done.13
  102.9 0.2 copy-done.15
  103.0 0.1 copy-done.19
  103.1 4.9 %all-to-all-start.2 = ((f32[32,40,128]{2,1,0:T(8,128)}), f32[32,40,128]{2,1,0:T(8,128)S(1)}, u32[]{:S(2)}, u32[]{:S(2)}) async-start(f32[32,40,128]{2,1,0:T(8,128)} %get-tuple-element.46), calls=%async_computation.2 | async-start | bytes 1310720 | tf_op jit(solution)/shard_map/all_to_all | solution.py:269
  108.1 1.0 copy-done.7
  109.2 1.2 copy-done.12
  110.4 1.0 copy-done.14
  111.4 1.0 copy-done.16
  112.5 0.9 copy-done.20
  113.4 3.2 %shard_map.92 = (f32[32,16,128]{2,1,0:T(8,128)S(1)}, f32[512,512]{1,0:T(8,128)S(1)}) custom-call(f32[512,256]{1,0:T(8,128)S(1)} %copy-done.7, f32[512,256]{1,0:T(8,128)S(1)} %copy-done.5, f32[512,512]{1,0:T(8,128)S(1)} %copy-done.12, f32[512,512]{1,0:T(8,128)S(1)} %get-tuple-element.27.feat_k, f32[256,512]{1,0:T(8,128)S(1)} %copy-done.14, ...), custom_call_target="tpu_custom_call" | custom-call | flops 4000000000 | bytes 1048576 | tf_op jit(solution)/shard_map/pallas_call | solution.py:257
  116.6 11.6 %all-to-all-done.2.got_ref = f32[32,40,128]{2,1,0:T(8,128)S(1)} async-done(((f32[32,40,128]{2,1,0:T(8,128)}), f32[32,40,128]{2,1,0:T(8,128)S(1)}, u32[]{:S(2)}, u32[]{:S(2)}) %all-to-all-start.2) | async-done | bytes 655392 | tf_op jit(solution)/shard_map/all_to_all | solution.py:269
  128.2 0.6 shard_map.93
  128.8 27.1 %all_to_all.25.got_ref = f32[32,48,128]{2,1,0:T(8,128)S(1)} all-to-all(f32[32,48,128]{2,1,0:T(8,128)S(1)} %get-tuple-element.48), channel_id=1, replica_groups=mesh['seq'=32,'head'=16] {'seq'}, dimensions={0} | all-to-all | bytes 1572864 | tf_op jit(solution)/shard_map/all_to_all | solution.py:269
  155.9 1.9 %shard_map.94 = (f32[32,16,128]{2,1,0:T(8,128)S(1)}, f32[8,256]{1,0:T(8,128)}) custom-call(f32[512,256]{1,0:T(8,128)S(1)} %copy-done.2, f32[512,256]{1,0:T(8,128)S(1)} %copy-done.5, f32[512,512]{1,0:T(8,128)S(1)} %get-tuple-element.27.feat_k, f32[512,512]{1,0:T(8,128)S(1)} %get-tuple-element.45.inner, f32[32,48,128]{2,1,0:T(8,128)S(1)} %all_to_all.25.got_ref, ...), custom_call_target="tpu_custom_call" | custom-call | flops 1000000000 | bytes 1048576 | tf_op jit(solution)/shard_map/pallas_call | solution.py:257
  157.8 16.0 %all_to_all.26.got_ref = f32[32,16,128]{2,1,0:T(8,128)S(1)} all-to-all(f32[32,16,128]{2,1,0:T(8,128)S(1)} %get-tuple-element.51), channel_id=1, replica_groups=mesh['seq'=32,'head'=16] {'seq'}, dimensions={0} | all-to-all | bytes 524288 | tf_op jit(solution)/shard_map/all_to_all | solution.py:269
  173.8 0.6 shard_map.95
  (37 shorter events, 0.1 us)
Async XLA Ops:
  0.6 1.0 copy-start.1
  1.7 1.0 copy-start.3
  2.7 0.9 copy-start.8
  6.7 13.4 %copy-start = (f32[32,4096]{1,0:T(8,128)S(1)}, f32[32,4096]{1,0:T(8,128)}, u32[]{:S(2)}) copy-start(f32[32,4096]{1,0:T(8,128)} %teacher_ref.3) | copy-start | bytes 1572868
  6.7 48.9 %all-to-all-start = ((f32[32,40,128]{2,1,0:T(8,128)}), f32[32,40,128]{2,1,0:T(8,128)S(1)}, u32[]{:S(2)}, u32[]{:S(2)}) async-start(f32[32,40,128]{2,1,0:T(8,128)} %get-tuple-element.29), calls=%async_computation | async-start | bytes 1310720 | tf_op jit(solution)/shard_map/all_to_all | solution.py:269
  20.6 3.4 %collective-permute-start = (f32[32,2048]{1,0:T(8,128)S(1)}, f32[32,2048]{1,0:T(8,128)S(1)}, u32[]{:S(2)}, u32[]{:S(2)}) collective-permute-start(f32[32,2048]{1,0:T(8,128)S(1)} %shard_map.88), channel_id=1, source_target_pairs={{0,1},{1,0},{2,3},{3,2},{4,5},{5,4},{6,7},{7,6},{8,9},{9,8},{10,11... | collective-permute-start | bytes 786440 | tf_op jit(solution)/shard_map/ppermute | solution.py:291
  24.7 26.6 %copy-start.23 = (s32[32,32]{1,0:T(8,128)S(1)}, s32[32,32]{1,0:T(8,128)}, u32[]{:S(2)}) copy-start(s32[32,32]{1,0:T(8,128)} %param.13) | copy-start | bytes 12292
  24.7 19.0 %collective-permute-start.1 = (f32[64,256]{1,0:T(8,128)S(1)}, f32[64,256]{1,0:T(8,128)S(1)}, u32[]{:S(2)}, u32[]{:S(2)}) collective-permute-start(f32[64,256]{1,0:T(8,128)S(1)} %get-tuple-element.31), channel_id=1, source_target_pairs={{0,2},{1,3},{2,4},{3,5},{4,6},{5,7},{6,8},{7,9},{8,10},{9,11},{10,... | collective-permute-start | bytes 196616 | tf_op jit(solution)/shard_map/ppermute | solution.py:299
  29.4 17.9 %collective-permute-start.2 = (f32[64,256]{1,0:T(8,128)S(1)}, f32[64,256]{1,0:T(8,128)S(1)}, u32[]{:S(2)}, u32[]{:S(2)}) collective-permute-start(f32[64,256]{1,0:T(8,128)S(1)} %get-tuple-element.32), channel_id=1, source_target_pairs={{0,4},{1,5},{2,6},{3,7},{4,8},{5,9},{6,10},{7,11},{8,12},{9,13},{1... | collective-permute-start | bytes 196616 | tf_op jit(solution)/shard_map/ppermute | solution.py:299
  32.1 19.2 %collective-permute-start.3 = (f32[64,256]{1,0:T(8,128)S(1)}, f32[64,256]{1,0:T(8,128)S(1)}, u32[]{:S(2)}, u32[]{:S(2)}) collective-permute-start(f32[64,256]{1,0:T(8,128)S(1)} %get-tuple-element.33), channel_id=1, source_target_pairs={{0,6},{1,7},{2,8},{3,9},{4,10},{5,11},{6,12},{7,13},{8,14},{9,15},... | collective-permute-start | bytes 196616 | tf_op jit(solution)/shard_map/ppermute | solution.py:299
  34.9 16.4 %collective-permute-start.4 = (f32[64,256]{1,0:T(8,128)S(1)}, f32[64,256]{1,0:T(8,128)S(1)}, u32[]{:S(2)}, u32[]{:S(2)}) collective-permute-start(f32[64,256]{1,0:T(8,128)S(1)} %get-tuple-element.34), channel_id=1, source_target_pairs={{0,8},{1,9},{2,10},{3,11},{4,12},{5,13},{6,14},{7,15},{8,0},{9,1},... | collective-permute-start | bytes 196616 | tf_op jit(solution)/shard_map/ppermute | solution.py:299
  41.8 12.0 %collective-permute-start.5 = (f32[64,256]{1,0:T(8,128)S(1)}, f32[64,256]{1,0:T(8,128)S(1)}, u32[]{:S(2)}, u32[]{:S(2)}) collective-permute-start(f32[64,256]{1,0:T(8,128)S(1)} %get-tuple-element.35), channel_id=1, source_target_pairs={{0,10},{1,11},{2,12},{3,13},{4,14},{5,15},{6,0},{7,1},{8,2},{9,3},... | collective-permute-start | bytes 196616 | tf_op jit(solution)/shard_map/ppermute | solution.py:299
  43.7 11.8 %collective-permute-start.6 = (f32[64,256]{1,0:T(8,128)S(1)}, f32[64,256]{1,0:T(8,128)S(1)}, u32[]{:S(2)}, u32[]{:S(2)}) collective-permute-start(f32[64,256]{1,0:T(8,128)S(1)} %get-tuple-element.36), channel_id=1, source_target_pairs={{0,12},{1,13},{2,14},{3,15},{4,0},{5,1},{6,2},{7,3},{8,4},{9,5},{1... | collective-permute-start | bytes 196616 | tf_op jit(solution)/shard_map/ppermute | solution.py:299
  47.3 8.3 %collective-permute-start.7 = (f32[64,256]{1,0:T(8,128)S(1)}, f32[64,256]{1,0:T(8,128)S(1)}, u32[]{:S(2)}, u32[]{:S(2)}) collective-permute-start(f32[64,256]{1,0:T(8,128)S(1)} %get-tuple-element.37), channel_id=1, source_target_pairs={{0,14},{1,15},{2,0},{3,1},{4,2},{5,3},{6,4},{7,5},{8,6},{9,7},{10,... | collective-permute-start | bytes 196616 | tf_op jit(solution)/shard_map/ppermute | solution.py:299
  57.2 10.1 %copy-start.4 = (f32[512,256]{1,0:T(8,128)S(1)}, f32[512,256]{1,0:T(8,128)}, u32[]{:S(2)}) copy-start(f32[512,256]{1,0:T(8,128)} %values.7) | copy-start | bytes 1572868
  57.2 10.1 %copy-start.6 = (f32[512,256]{1,0:T(8,128)S(1)}, f32[512,256]{1,0:T(8,128)}, u32[]{:S(2)}) copy-start(f32[512,256]{1,0:T(8,128)} %queries.3) | copy-start | bytes 1572868
  57.2 10.1 %copy-start.9 = (f32[1,256,256]{2,1,0:T(8,128)S(1)}, f32[1,256,256]{2,1,0:T(8,128)}, u32[]{:S(2)}) copy-start(f32[1,256,256]{2,1,0:T(8,128)} %param.11) | copy-start | bytes 786436
  57.2 38.2 %all-to-all-start.1 = ((f32[32,64,128]{2,1,0:T(8,128)}), f32[32,64,128]{2,1,0:T(8,128)S(1)}, u32[]{:S(2)}, u32[]{:S(2)}) async-start(f32[32,64,128]{2,1,0:T(8,128)} %get-tuple-element.38), calls=%async_computation.1 | async-start | bytes 2097152 | tf_op jit(solution)/shard_map/all_to_all | solution.py:269
  70.3 1.0 copy-start.10
  71.3 0.8 copy-start.17
  72.1 0.7 copy-start.21
  95.5 1.2 copy-start.11
  96.7 1.0 copy-start.18
  97.7 0.9 copy-start.22
  102.1 0.8 copy-start.13
  102.1 1.0 copy-start.15
  102.1 1.1 copy-start.19
  102.1 6.0 %copy-start.5 = (f32[512,256]{1,0:T(8,128)S(1)}, f32[512,256]{1,0:T(8,128)}, u32[]{:S(2)}) copy-start(f32[512,256]{1,0:T(8,128)} %values.7) | copy-start | bytes 1572868
  103.1 25.0 %all-to-all-start.2 = ((f32[32,40,128]{2,1,0:T(8,128)}), f32[32,40,128]{2,1,0:T(8,128)S(1)}, u32[]{:S(2)}, u32[]{:S(2)}) async-start(f32[32,40,128]{2,1,0:T(8,128)} %get-tuple-element.46), calls=%async_computation.2 | async-start | bytes 1310720 | tf_op jit(solution)/shard_map/all_to_all | solution.py:269
  108.1 1.0 copy-start.7
  109.1 1.2 copy-start.12
  110.4 1.0 copy-start.14
  111.4 1.0 copy-start.16
  112.5 0.9 copy-start.20
  128.8 27.1 %copy-start.2 = (f32[512,256]{1,0:T(8,128)S(1)}, f32[512,256]{1,0:T(8,128)}, u32[]{:S(2)}) copy-start(f32[512,256]{1,0:T(8,128)} %keys.3) | copy-start | bytes 1572868

commit v3 on v2

--- a/solution.py
+++ b/solution.py
@@ -9,8 +9,6 @@
 
 exact_prec = lax.Precision.HIGHEST
 LANES = 128
-CORES = 2
-HEAD_WIDTH = 256
 ROWS = 8
 NN = (((1,), (0,)), ((), ()))
 NT = (((1,), (1,)), ((), ()))
@@ -75,24 +73,26 @@
     pack_norm(out_ref, width * ROWS, jnp.sum(feat, axis=0, keepdims=True))
 
 
-def query_kernel(queries, weights, feat_k, values, feat_ref, numer_ref, raw_ref):
+def query_kernel(queries, weights, feat_k, values, out_ref):
     half = weights.shape[1]
-    tokens = queries.shape[0]
+    tokens, width = queries.shape
+    feats = 2 * half
     step = 256
     first, second = features(queries[...], weights[...])
-    feat_ref[:, :half] = first
-    feat_ref[:, half:] = second
+    out_ref[:, :half] = first
+    out_ref[:, half:feats] = second
     vals = halves(values[...])
     keys = halves(feat_k[...])
     for lo in range(0, tokens, step):
         hi = lo + step
-        fq = halves(feat_ref[lo:hi, :])
+        fq = halves(out_ref[lo:hi, :feats])
         scores = dot3(fq, (keys[0][:hi], keys[1][:hi]), NT)
         t = lax.broadcasted_iota(jnp.int32, scores.shape, 0) + lo
         s = lax.broadcasted_iota(jnp.int32, scores.shape, 1)
         scores = jnp.where(t >= s, scores, 0.0)
-        raw_ref[lo:hi, :] = jnp.sum(scores, axis=-1, keepdims=True)
-        numer_ref[lo:hi, :] = dot3(halves(scores), (vals[0][:hi], vals[1][:hi]), NN)
+        raw = jnp.sum(scores, axis=-1, keepdims=True)
+        out_ref[lo:hi, feats + width :] = jnp.broadcast_to(raw, (step, LANES))
+        out_ref[lo:hi, feats : feats + width] = dot3(halves(scores), (vals[0][:hi], vals[1][:hi]), NN)
 
 
 def scan_kernel(backward, state_rows, mine_ref, got_ref, out_ref, norm_ref):
@@ -109,48 +109,14 @@
     norm_ref[...] = norm
 
 
-def partner_kernel(place_ref, teacher_ref, out_ref):
-    other = 1 - place_ref[1] % CORES
-    width = teacher_ref.shape[1] // place_count(teacher_ref)
-    for pair in range(place_count(teacher_ref) // CORES):
-        at = pl.multiple_of((pair * CORES + other) * width, width)
-        out_ref[:, pair * width : (pair + 1) * width] = teacher_ref[:, pl.ds(at, width)]
-
-
-def place_count(teacher_ref):
-    return teacher_ref.shape[1] // HEAD_WIDTH
-
-
-def spread_kernel(place_ref, teacher_ref, got_ref, *out_refs):
-    core = place_ref[1] % CORES
-    chip = place_ref[1] // CORES
-    rows = teacher_ref.shape[0]
-    ring = len(out_refs)
-    mine = pl.multiple_of(core * rows, rows)
-    theirs = pl.multiple_of((1 - core) * rows, rows)
-    for k, out_ref in enumerate(out_refs):
-        to = (chip + k) % ring
-        at = pl.multiple_of((to * CORES + core) * HEAD_WIDTH, HEAD_WIDTH)
-        out_ref[pl.ds(mine, rows), :] = teacher_ref[:, pl.ds(at, HEAD_WIDTH)]
-        at = pl.multiple_of(to * HEAD_WIDTH, HEAD_WIDTH)
-        out_ref[pl.ds(theirs, rows), :] = got_ref[:, pl.ds(at, HEAD_WIDTH)]
-
-
-def forward_scan_kernel(state_rows, rows, place_ref, owner_ref, got_ref, *refs):
-    blocks_refs, (out_ref, norm_ref) = refs[:-2], refs[-2:]
-    scan_kernel(False, state_rows, place_ref, got_ref, out_ref, norm_ref)
-    ring = len(blocks_refs)
-    chip = place_ref[1] // CORES
-    for k, blocks_ref in enumerate(blocks_refs):
-        source = (chip + ring - k) % ring
-        each = blocks_ref.shape[0] // rows
-        for m in range(each):
-            owner = owner_ref[source * each + m]
-            for c in range(HEAD_WIDTH // LANES):
-                base = state_rows + c * rows
-                out_ref[owner, base : base + rows, :] = blocks_ref[
-                    m * rows : (m + 1) * rows, c * LANES : (c + 1) * LANES
-                ]
+def forward_scan_kernel(state_rows, mine_ref, owner_ref, got_ref, blocks_ref, out_ref, norm_ref):
+    scan_kernel(False, state_rows, mine_ref, got_ref, out_ref, norm_ref)
+    count, rows, width = blocks_ref.shape
+    for place in range(count):
+        owner = owner_ref[place]
+        for c in range(width // LANES):
+            base = state_rows + c * rows
+            out_ref[owner, base : base + rows, :] = blocks_ref[place, :, c * LANES : (c + 1) * LANES]
 
 
 def backward_scan_kernel(state_rows, mine_ref, got_ref, term_ref, out_ref, norm_ref):
@@ -163,16 +129,13 @@
 
 
 def middle_kernel(
-    block_rows, within_ref, got_ref, norm_ref, feat_q, numer, raw,
-    state_ref, grad_ref, div_ref, out_ref, teacher_ref,
+    block_rows, feats, within_ref, got_ref, norm_ref, block_ref, grad_ref, out_ref, teacher_ref
 ):
-    feats = feat_q.shape[1]
-    width = numer.shape[1]
+    width = teacher_ref.shape[1]
     count = got_ref.shape[0]
     chunks = feats // LANES
     state_rows = chunks * ROWS
     state = unpack(got_ref, 0, chunks)
-    state_ref[...] = state
     for source in range(count):
         at = pl.multiple_of(within_ref[source] * block_rows, block_rows)
         for c in range(width // LANES):
@@ -180,18 +143,18 @@
             teacher_ref[pl.ds(at, block_rows), c * LANES : (c + 1) * LANES] = got_ref[
                 source, base : base + block_rows, :
             ]
-    fq = feat_q[...]
+    fq = block_ref[:, :feats]
     fq_pair = halves(fq)
-    numerator = numer[...] + dot3(fq_pair, halves(state), NT)
+    numerator = block_ref[:, feats : feats + width] + dot3(fq_pair, halves(state), NT)
     prev_norm = norm_row(norm_ref, chunks)
-    raw_sum = raw[...] + jnp.sum(fq * prev_norm, axis=-1, keepdims=True)
+    raw_sum = block_ref[:, feats + width : feats + width + 1] + jnp.sum(fq * prev_norm, axis=-1, keepdims=True)
     divisor = jnp.maximum(raw_sum, 1.0)
     student = numerator / divisor
     mismatch = student - teacher_ref[...]
     grad_num = mismatch / divisor
     grad_div = jnp.where(raw_sum > 1.0, -jnp.sum(mismatch * student, axis=-1, keepdims=True) / divisor, 0.0)
-    grad_ref[...] = grad_num
-    div_ref[...] = grad_div
+    grad_ref[:, :width] = grad_num
+    grad_ref[:, width:] = jnp.broadcast_to(grad_div, (grad_div.shape[0], LANES))
     pack(out_ref, 0, dot3(halves(grad_num), fq_pair, TN))
     pack_norm(out_ref, state_rows, jnp.sum(grad_div * fq, axis=0, keepdims=True))
 
@@ -205,21 +168,22 @@
 
 
 def weight_kernel(
-    queries, values, feat_q, feat_k, state, norm_ref, grad_num, grad_div, term_ref, inner_ref, pre_ref
+    queries, values, block_ref, feat_k, got_ref, norm_ref, grad_ref, term_ref, inner_ref, pre_ref
 ):
-    tokens, feats = feat_q.shape
+    tokens, feats = feat_k.shape
+    width = values.shape[1]
     half = feats // 2
     step = 256
     chunks = feats // LANES
     vals = halves(values[...])
     keys = halves(feat_k[...])
-    states = halves(state[...])
+    states = halves(unpack(got_ref, 0, chunks))
     prev_norm = norm_row(norm_ref, chunks)
     for lo in range(0, tokens, step):
         hi = lo + step
-        div = grad_div[lo:hi, :]
-        num = halves(grad_num[lo:hi, :])
-        fq = feat_q[lo:hi, :]
+        div = grad_ref[lo:hi, width : width + 1]
+        num = halves(grad_ref[lo:hi, :width])
+        fq = block_ref[lo:hi, :feats]
         weights = dot3(num, (vals[0][:hi], vals[1][:hi]), NT) + div
         t = lax.broadcasted_iota(jnp.int32, weights.shape, 0) + lo
         s = lax.broadcasted_iota(jnp.int32, weights.shape, 1)
@@ -275,49 +239,42 @@
     feats = 2 * half
     count = lax.axis_size("seq")
     mine = lax.axis_index("seq")
-    heads = lax.axis_size("head")
     chunks = feats // LANES
     state_rows = chunks * ROWS
     block_rows = tokens // count
     term_rows = half // LANES * ROWS
 
-    place = jnp.stack([mine, lax.axis_index("head")]).astype(jnp.int32)
+    place = mine.astype(jnp.int32).reshape(1)
     slot_ids = lax.dynamic_index_in_dim(block_map, mine, 0, keepdims=False)
     owner_ids = slot_ids // count
     within = jnp.sum(jnp.where(block_map // count == mine, block_map % count, 0), axis=1).astype(jnp.int32)
-    ring = heads // CORES
-    rows = teacher_out.shape[0]
-    (partner,) = call(partner_kernel, [(rows, ring * width)], "sv", 0.1, (place, teacher_out))
-    partner = lax.ppermute(partner, "head", [(h, h ^ 1) for h in range(heads)])
+    gathered = lax.all_to_all(teacher_out, "head", split_axis=1, concat_axis=0, tiled=True)
+    blocks = gathered.reshape(count, block_rows, width)
+
     feat_k, out1 = call(
         key_kernel, [(tokens, feats), (count, state_rows + ROWS, LANES)], "vvv", 1.0,
         (keys, key_map[0], values),
     )
     got1 = exchange(out1, "seq")
-    blocks = call(spread_kernel, [(CORES * rows, width)] * ring, "svv", 0.1, (place, teacher_out, partner))
-    blocks = list(blocks[:1]) + [
-        lax.ppermute(blocks[k], "head", [(h, (h + CORES * k) % heads) for h in range(heads)])
-        for k in range(1, ring)
-    ]
-    feat_q, numer, raw = call(
-        query_kernel, [(tokens, feats), (tokens, width), (tokens, 1)], "vvvv", 2.0,
+    (block,) = call(
+        query_kernel, [(tokens, feats + width + LANES)], "vvvv", 2.0,
         (queries, query_map[0], feat_k, values),
     )
     out2, prev_norm = call(
-        functools.partial(forward_scan_kernel, state_rows, block_rows),
+        functools.partial(forward_scan_kernel, state_rows),
         [(count, state_rows + block_rows * (width // LANES), LANES), (ROWS, LANES)],
-        "ssv" + "v" * ring, 0.1, (place, owner_ids, got1, *blocks),
+        "ssvv", 0.1, (place, owner_ids, got1, blocks),
     )
     got2 = exchange(out2, "seq")
-    state, grad_num, grad_div, out3 = call(
-        functools.partial(middle_kernel, block_rows),
-        [(width, feats), (tokens, width), (tokens, 1), (count, state_rows + ROWS, LANES)],
-        "svvvvv", 1.0, (within, got2, prev_norm, feat_q, numer, raw), [(tokens, width)],
+    grads, out3 = call(
+        functools.partial(middle_kernel, block_rows, feats),
+        [(tokens, width + LANES), (count, state_rows + ROWS, LANES)],
+        "svvv", 1.0, (within, got2, prev_norm, block), [(tokens, width)],
     )
     got3 = exchange(out3, "seq")
     term_q, inner = call(
-        weight_kernel, [(count, term_rows, LANES), (tokens, feats)], "vvvvvvvv", 4.0,
-        (queries, values, feat_q, feat_k, state, prev_norm, grad_num, grad_div), [(tokens, half)],
+        weight_kernel, [(count, term_rows, LANES), (tokens, feats)], "vvvvvvv", 4.0,
+        (queries, values, block, feat_k, got2, prev_norm, grads), [(tokens, half)],
     )
     out4, next_norm = call(
         functools.partial(backward_scan_kernel, state_rows),

time: 176 us -> 172 us (0.977)
  the two profiles are of different devices: /device:TPU:24 before, /device:TPU:64 now
where the time goes in v3:
time: 172 us
  waiting for transfers between devices  67.7 us (39%)
  blocking collectives  43.4 us (25%)
  starting transfers between devices  30.9 us (18%)
  Pallas kernels  16.8 us (10%)
  local copies, waits for them, and re-layouts  11.1 us (6%)
    all_to_all x3, waiting for transfers between devices, exchange(): return lax.all_to_all(value, axis, split_axis=0, concat_axis=0, tiled=True)  54.8 us
    all_to_all x2, blocking collectives, exchange(): return lax.all_to_all(value, axis, split_axis=0, concat_axis=0, tiled=True)  43.4 us
    all_to_all x3, starting transfers between devices, exchange(): return lax.all_to_all(value, axis, split_axis=0, concat_axis=0, tiled=True)  23.7 us
    pallas_call x8, Pallas kernels, call(): pl.pallas_call(body, out_shape=[jax.ShapeDtypeStruct(shape, jnp.float32)...  16.8 us
    all_to_all x1, waiting for transfers between devices, per_device(): lax.all_to_all(teacher_out, 'head', split_axis=1, concat_axis=0, tiled=True)  12.9 us
    unnamed x34, local copies, waits for them, and re-layouts  9.11 us
    all_to_all x1, starting transfers between devices, per_device(): lax.all_to_all(teacher_out, 'head', split_axis=1, concat_axis=0, tiled=True)  7.21 us
  transfers between devices with their start and end apart: 4, of which 4 were waited for; matrix products, arithmetic and copies ran while one was open for 1% of the time, Pallas kernels for 5%

profile of v3, /device:TPU:64, one launch (start us, length us, event | category | flops | bytes accessed | tf_op | source)
XLA Modules:
  0.0 171.6 jit_solution(15598160345963304457)
XLA Ops:
  0.6 0.0 copy-start.4
  0.6 0.0 copy-start.2
  0.7 0.0 copy-start.9
  0.7 2.0 %copy.12 = f32[4,16,8,256]{3,2,0,1:T(8,128)} copy(f32[4,16,8,256]{3,2,1,0:T(8,128)} %bitcast.23) | data formatting | bytes 1048576 | tf_op jit(solution)/shard_map/all_to_all | solution.py:251
  2.7 7.2 %all-to-all-start.1 = ((f32[32,16,256]{2,0,1:T(8,128)}), f32[32,16,256]{2,0,1:T(8,128)S(1)}, u32[]{:S(2)}, u32[]{:S(2)}) async-start(f32[32,16,256]{2,0,1:T(8,128)} %bitcast.19), calls=%async_computation.1 | async-start | bytes 1048576 | tf_op jit(solution)/shard_map/all_to_all | solution.py:251
  9.9 0.0 copy-done.4
  9.9 0.0 copy-done.2
  9.9 0.0 copy-done.9
  9.9 3.0 %shard_map.86 = (f32[512,512]{1,0:T(8,128)S(1)}, f32[32,40,128]{2,1,0:T(8,128)}) custom-call(f32[512,256]{1,0:T(8,128)S(1)} %copy-done.2, f32[256,256]{1,0:T(8,128)S(1)} %bitcast.21, f32[512,256]{1,0:T(8,128)S(1)} %copy-done.4), custom_call_target="tpu_custom_call" | custom-call | flops 1000000000 | bytes 1048576 | tf_op jit(solution)/shard_map/pallas_call | solution.py:221
  12.9 12.9 %all-to-all-done.1 = f32[32,16,256]{2,0,1:T(8,128)S(1)} async-done(((f32[32,16,256]{2,0,1:T(8,128)}), f32[32,16,256]{2,0,1:T(8,128)S(1)}, u32[]{:S(2)}, u32[]{:S(2)}) %all-to-all-start.1) | async-done | bytes 524320 | tf_op jit(solution)/shard_map/all_to_all | solution.py:251
  25.8 12.6 %all-to-all-start = ((f32[32,40,128]{2,1,0:T(8,128)}), f32[32,40,128]{2,1,0:T(8,128)S(1)}, u32[]{:S(2)}, u32[]{:S(2)}) async-start(f32[32,40,128]{2,1,0:T(8,128)} %get-tuple-element.15), calls=%async_computation | async-start | bytes 1310720 | tf_op jit(solution)/shard_map/all_to_all | solution.py:233
  38.4 0.0 copy-start.7
  38.4 0.0 copy-start.10
  38.4 0.8 and_select_fusion.owner_ref
  39.2 19.8 %all-to-all-done.got_ref = f32[32,40,128]{2,1,0:T(8,128)S(1)} async-done(((f32[32,40,128]{2,1,0:T(8,128)}), f32[32,40,128]{2,1,0:T(8,128)S(1)}, u32[]{:S(2)}, u32[]{:S(2)}) %all-to-all-start) | async-done | bytes 655392 | tf_op jit(solution)/shard_map/all_to_all | solution.py:233
  59.1 1.6 shard_map.88
  60.7 0.0 copy-start.16
  60.7 5.9 %all-to-all-start.2 = ((f32[32,64,128]{2,1,0:T(8,128)}), f32[32,64,128]{2,1,0:T(8,128)S(1)}, u32[]{:S(2)}, u32[]{:S(2)}) async-start(f32[32,64,128]{2,1,0:T(8,128)} %get-tuple-element.16), calls=%async_computation.2 | async-start | bytes 2097152 | tf_op jit(solution)/shard_map/all_to_all | solution.py:233
  66.6 0.0 copy-done.16
  66.6 0.1 fusion.2.within_ref
  66.7 0.0 copy-done.7
  66.7 0.0 copy-done.10
  66.8 3.0 %shard_map.87.block_ref = f32[512,896]{1,0:T(8,128)S(1)} custom-call(f32[512,256]{1,0:T(8,128)S(1)} %copy-done.7, f32[256,256]{1,0:T(8,128)S(1)} %bitcast.22, f32[512,512]{1,0:T(8,128)S(1)} %get-tuple-element.14.feat_k, f32[512,256]{1,0:T(8,128)S(1)} %copy-done.4), custom_call_target="tpu_custom_call" | custom-call | flops 2000000000 | bytes 1048576 | tf_op jit(solution)/shard_map/pallas_call | solution.py:221
  69.8 0.0 copy-start.11
  69.8 1.2 copy-done.11
  71.0 24.4 %all-to-all-done.2.got_ref = f32[32,64,128]{2,1,0:T(8,128)S(1)} async-done(((f32[32,64,128]{2,1,0:T(8,128)}), f32[32,64,128]{2,1,0:T(8,128)S(1)}, u32[]{:S(2)}, u32[]{:S(2)}) %all-to-all-start.2) | async-done | bytes 1048608 | tf_op jit(solution)/shard_map/all_to_all | solution.py:233
  95.4 0.0 copy-start
  95.4 1.9 %copy-done.12 = f32[512,896]{1,0:T(8,128)S(1)} copy-done((f32[512,896]{1,0:T(8,128)S(1)}, f32[512,896]{1,0:T(8,128)}, u32[]{:S(2)}) %copy-start.12) | copy-done | bytes 1835032
  97.3 3.4 %shard_map.89 = (f32[512,384]{1,0:T(8,128)S(1)}, f32[32,40,128]{2,1,0:T(8,128)}) custom-call(s32[32]{0:T(128)S(1)} %fusion.2.within_ref, f32[32,64,128]{2,1,0:T(8,128)S(1)} %all-to-all-done.2.got_ref, f32[8,128]{1,0:T(8,128)S(1)} %get-tuple-element.17.norm_ref, f32[512,896]{1,0:T(8,128)S(1)} %copy-done.12), custom_call_target="tpu_custom_call" | custom-call | flops 1000000000 | bytes 1048576 | tf_op jit(solution)/shard_map/pallas_call | solution.py:221
  100.6 0.0 copy-done
  100.7 5.2 %all-to-all-start.3 = ((f32[32,40,128]{2,1,0:T(8,128)}), f32[32,40,128]{2,1,0:T(8,128)S(1)}, u32[]{:S(2)}, u32[]{:S(2)}) async-start(f32[32,40,128]{2,1,0:T(8,128)} %get-tuple-element.20), calls=%async_computation.3 | async-start | bytes 1310720 | tf_op jit(solution)/shard_map/all_to_all | solution.py:233
  105.9 0.0 copy-done.14
  105.9 0.0 copy-start.1
  105.9 1.2 copy-done.1
  107.1 1.0 copy-done.5
  108.1 1.0 copy-done.8
  109.2 1.5 copy-done.13
  110.7 1.1 copy-done.15
  111.8 3.2 %shard_map.90 = (f32[32,16,128]{2,1,0:T(8,128)S(1)}, f32[512,512]{1,0:T(8,128)S(1)}) custom-call(f32[512,256]{1,0:T(8,128)S(1)} %copy-done.8, f32[512,256]{1,0:T(8,128)S(1)} %copy-done.5, f32[512,896]{1,0:T(8,128)S(1)} %copy-done.13, f32[512,512]{1,0:T(8,128)S(1)} %get-tuple-element.14.feat_k, f32[32,64,128]{2,1,0:T(8,128)S(1)} %copy-done.1, ...), custom_call_target="tpu_custom_call" | custom-call | flops 4000000000 | bytes 1048576 | tf_op jit(solution)/shard_map/pallas_call | solution.py:221
  115.0 0.0 copy-start.3
  115.0 10.6 %all-to-all-done.3.got_ref = f32[32,40,128]{2,1,0:T(8,128)S(1)} async-done(((f32[32,40,128]{2,1,0:T(8,128)}), f32[32,40,128]{2,1,0:T(8,128)S(1)}, u32[]{:S(2)}, u32[]{:S(2)}) %all-to-all-start.3) | async-done | bytes 655392 | tf_op jit(solution)/shard_map/all_to_all | solution.py:233
  125.6 0.1 shard_map.91
  125.6 27.3 %all_to_all.41.got_ref = f32[32,48,128]{2,1,0:T(8,128)S(1)} all-to-all(f32[32,48,128]{2,1,0:T(8,128)S(1)} %get-tuple-element.22), channel_id=1, replica_groups=mesh['seq'=32,'head'=16] {'seq'}, dimensions={0} | all-to-all | bytes 1572864 | tf_op jit(solution)/shard_map/all_to_all | solution.py:233
  152.9 0.0 copy-done.3
  152.9 0.0 copy-done.6
  152.9 1.9 %shard_map.92 = (f32[32,16,128]{2,1,0:T(8,128)S(1)}, f32[8,256]{1,0:T(8,128)}) custom-call(f32[512,256]{1,0:T(8,128)S(1)} %copy-done.3, f32[512,256]{1,0:T(8,128)S(1)} %copy-done.6, f32[512,512]{1,0:T(8,128)S(1)} %get-tuple-element.14.feat_k, f32[512,512]{1,0:T(8,128)S(1)} %get-tuple-element.19.inner, f32[32,48,128]{2,1,0:T(8,128)S(1)} %all_to_all.41.got_ref, ...), custom_call_target="tpu_custom_call" | custom-call | flops 1000000000 | bytes 1048576 | tf_op jit(solution)/shard_map/pallas_call | solution.py:221
  154.8 16.1 %all_to_all.42.got_ref = f32[32,16,128]{2,1,0:T(8,128)S(1)} all-to-all(f32[32,16,128]{2,1,0:T(8,128)S(1)} %get-tuple-element.25), channel_id=1, replica_groups=mesh['seq'=32,'head'=16] {'seq'}, dimensions={0} | all-to-all | bytes 524288 | tf_op jit(solution)/shard_map/all_to_all | solution.py:233
  170.9 0.6 shard_map.93
  (7 shorter events, 0.0 us)
Async XLA Ops:
  0.6 9.3 %copy-start.4 = (f32[512,256]{1,0:T(8,128)S(1)}, f32[512,256]{1,0:T(8,128)}, u32[]{:S(2)}) copy-start(f32[512,256]{1,0:T(8,128)} %values.7) | copy-start | bytes 1572868
  0.6 9.3 %copy-start.2 = (f32[512,256]{1,0:T(8,128)S(1)}, f32[512,256]{1,0:T(8,128)}, u32[]{:S(2)}) copy-start(f32[512,256]{1,0:T(8,128)} %keys.3) | copy-start | bytes 1572868
  0.7 9.3 %copy-start.9 = (f32[1,256,256]{2,1,0:T(8,128)S(1)}, f32[1,256,256]{2,1,0:T(8,128)}, u32[]{:S(2)}) copy-start(f32[1,256,256]{2,1,0:T(8,128)} %param.12) | copy-start | bytes 786436
  2.7 23.2 %all-to-all-start.1 = ((f32[32,16,256]{2,0,1:T(8,128)}), f32[32,16,256]{2,0,1:T(8,128)S(1)}, u32[]{:S(2)}, u32[]{:S(2)}) async-start(f32[32,16,256]{2,0,1:T(8,128)} %bitcast.19), calls=%async_computation.1 | async-start | bytes 1048576 | tf_op jit(solution)/shard_map/all_to_all | solution.py:251
  25.8 33.2 %all-to-all-start = ((f32[32,40,128]{2,1,0:T(8,128)}), f32[32,40,128]{2,1,0:T(8,128)S(1)}, u32[]{:S(2)}, u32[]{:S(2)}) async-start(f32[32,40,128]{2,1,0:T(8,128)} %get-tuple-element.15), calls=%async_computation | async-start | bytes 1310720 | tf_op jit(solution)/shard_map/all_to_all | solution.py:233
  38.4 28.3 %copy-start.7 = (f32[512,256]{1,0:T(8,128)S(1)}, f32[512,256]{1,0:T(8,128)}, u32[]{:S(2)}) copy-start(f32[512,256]{1,0:T(8,128)} %queries.3) | copy-start | bytes 1572868
  38.4 28.3 %copy-start.10 = (f32[1,256,256]{2,1,0:T(8,128)S(1)}, f32[1,256,256]{2,1,0:T(8,128)}, u32[]{:S(2)}) copy-start(f32[1,256,256]{2,1,0:T(8,128)} %param.11) | copy-start | bytes 786436
  60.7 6.0 %copy-start.16 = (s32[32,32]{1,0:T(8,128)S(1)}, s32[32,32]{1,0:T(8,128)}, u32[]{:S(2)}) copy-start(s32[32,32]{1,0:T(8,128)} %param.13) | copy-start | bytes 12292
  60.7 34.7 %all-to-all-start.2 = ((f32[32,64,128]{2,1,0:T(8,128)}), f32[32,64,128]{2,1,0:T(8,128)S(1)}, u32[]{:S(2)}, u32[]{:S(2)}) async-start(f32[32,64,128]{2,1,0:T(8,128)} %get-tuple-element.16), calls=%async_computation.2 | async-start | bytes 2097152 | tf_op jit(solution)/shard_map/all_to_all | solution.py:233
  69.8 1.3 copy-start.11
  95.4 5.3 %copy-start = (f32[32,64,128]{2,1,0:T(8,128)}, f32[32,64,128]{2,1,0:T(8,128)S(1)}, u32[]{:S(2)}) copy-start(f32[32,64,128]{2,1,0:T(8,128)S(1)} %all-to-all-done.2.got_ref) | copy-start | bytes 3145732
  95.4 1.9 %copy-start.12 = (f32[512,896]{1,0:T(8,128)S(1)}, f32[512,896]{1,0:T(8,128)}, u32[]{:S(2)}) copy-start(f32[512,896]{1,0:T(8,128)} %copy-done.11) | copy-start | bytes 5505028
  100.7 5.2 %copy-start.14 = (f32[512,384]{1,0:T(8,128)}, f32[512,384]{1,0:T(8,128)S(1)}, u32[]{:S(2)}) copy-start(f32[512,384]{1,0:T(8,128)S(1)} %get-tuple-element.18.grad_ref) | copy-start | bytes 2359300
  100.7 24.9 %all-to-all-start.3 = ((f32[32,40,128]{2,1,0:T(8,128)}), f32[32,40,128]{2,1,0:T(8,128)S(1)}, u32[]{:S(2)}, u32[]{:S(2)}) async-start(f32[32,40,128]{2,1,0:T(8,128)} %get-tuple-element.20), calls=%async_computation.3 | async-start | bytes 1310720 | tf_op jit(solution)/shard_map/all_to_all | solution.py:233
  105.9 1.2 copy-start.1
  107.1 1.0 copy-start.5
  108.1 1.0 copy-start.8
  109.2 1.5 copy-start.13
  110.7 1.1 copy-start.15
  115.0 37.9 %copy-start.3 = (f32[512,256]{1,0:T(8,128)S(1)}, f32[512,256]{1,0:T(8,128)}, u32[]{:S(2)}) copy-start(f32[512,256]{1,0:T(8,128)} %keys.3) | copy-start | bytes 1572868
  125.6 27.4 %copy-start.6 = (f32[512,256]{1,0:T(8,128)S(1)}, f32[512,256]{1,0:T(8,128)}, u32[]{:S(2)}) copy-start(f32[512,256]{1,0:T(8,128)} %values.7) | copy-start | bytes 1572868

commit v4 on v3

--- a/solution.py
+++ b/solution.py
@@ -7,8 +7,10 @@
 from jax.experimental.pallas import tpu as pltpu
 from jax.sharding import PartitionSpec as P
 
+
 exact_prec = lax.Precision.HIGHEST
 LANES = 128
+NORM_ROWS = 4
 ROWS = 8
 NN = (((1,), (0,)), ((), ()))
 NT = (((1,), (1,)), ((), ()))
@@ -52,28 +54,79 @@
     return jnp.concatenate(parts, axis=-1)
 
 
-def pack_norm(out_ref, base, norm):
-    owners = out_ref.shape[0]
+def norm_tile(norm):
     count = norm.shape[1] // LANES
     rows = [norm[:, c * LANES : (c + 1) * LANES] for c in range(count)]
     rows.append(jnp.zeros((ROWS - count, LANES), jnp.float32))
-    tile = jnp.concatenate(rows, axis=0)
+    return jnp.concatenate(rows, axis=0)
+
+
+def pack_norm(out_ref, base, norm):
+    owners = out_ref.shape[0]
+    tile = norm_tile(norm)
     out_ref[:, base : base + ROWS, :] = jnp.broadcast_to(tile[None], (owners, ROWS, LANES))
 
 
-def key_kernel(keys, weights, values, feat_ref, out_ref):
+def key_kernel(place_ref, keys, weights, values, feat_ref, send_ref, keep_ref):
     half = weights.shape[1]
     first, second = features(keys[...], weights[...])
     feat_ref[:, :half] = first
     feat_ref[:, half:] = second
     feat = feat_ref[...]
     state = dot3(halves(values[...]), halves(feat), TN)
-    width = state.shape[1] // LANES
-    pack(out_ref, 0, state)
-    pack_norm(out_ref, width * ROWS, jnp.sum(feat, axis=0, keepdims=True))
-
-
-def query_kernel(queries, weights, feat_k, values, out_ref):
+    split = state.shape[0] // 2
+    odd = place_ref[0] % 2 == 1
+    low, high = state[:split], state[split:]
+    slices = split // ROWS
+    norm = norm_tile(jnp.sum(feat, axis=0, keepdims=True))
+    for ref, value in ((send_ref, jnp.where(odd, low, high)), (keep_ref, jnp.where(odd, high, low))):
+        for c in range(value.shape[1] // LANES):
+            part = value[:, c * LANES : (c + 1) * LANES]
+            ref[:slices, c * ROWS : (c + 1) * ROWS, :] = part.reshape(slices, ROWS, LANES)
+        ref[slices, :ROWS, :] = norm
+        ref[slices, ROWS:, :] = jnp.zeros_like(ref[slices, ROWS:, :])
+
+
+def pair_kernel(place_ref, keep_ref, got_ref, out_ref):
+    slices, rows, _ = out_ref.shape
+    rows -= ROWS
+    odd = place_ref[0] % 2 == 1
+    out_ref[:, :rows, :] = keep_ref[:slices] + got_ref[:slices]
+    mine, other = keep_ref[slices, :NORM_ROWS, :], got_ref[slices, :NORM_ROWS, :]
+    tile = jnp.concatenate([jnp.where(odd, other, mine), jnp.where(odd, mine, other)], axis=0)
+    out_ref[:, rows:, :] = jnp.broadcast_to(tile[None], (slices, ROWS, LANES))
+
+
+def unpack_half(ref):
+    slices = ref.shape[0] - 1
+    return jnp.concatenate(
+        [
+            ref[:slices, c * ROWS : (c + 1) * ROWS, :].reshape(slices * ROWS, LANES)
+            for c in range(ref.shape[1] // ROWS)
+        ],
+        axis=-1,
+    )
+
+
+def even_state(place_ref, low_ref, high_ref):
+    odd = place_ref[0] % 2 == 1
+    both = jnp.concatenate([unpack_half(low_ref), unpack_half(high_ref)], axis=0)
+    return jnp.where(odd, both, 0.0)
+
+
+def unpack_pairs(ref, count):
+    pairs = ref.shape[0] // 2
+    halves_of = []
+    for parity in range(2):
+        parts = []
+        for c in range(count):
+            part = ref[:, c * ROWS : (c + 1) * ROWS, :].reshape(pairs, 2, ROWS, LANES)
+            parts.append(part[:, parity].reshape(pairs * ROWS, LANES))
+        halves_of.append(jnp.concatenate(parts, axis=-1))
+    return jnp.concatenate(halves_of, axis=0)
+
+
+def query_kernel(place_ref, queries, weights, feat_k, values, low_ref, high_ref, out_ref):
     half = weights.shape[1]
     tokens, width = queries.shape
     feats = 2 * half
@@ -83,6 +136,7 @@
     out_ref[:, half:feats] = second
     vals = halves(values[...])
     keys = halves(feat_k[...])
+    before = halves(even_state(place_ref, low_ref, high_ref))
     for lo in range(0, tokens, step):
         hi = lo + step
         fq = halves(out_ref[lo:hi, :feats])
@@ -92,25 +146,26 @@
         scores = jnp.where(t >= s, scores, 0.0)
         raw = jnp.sum(scores, axis=-1, keepdims=True)
         out_ref[lo:hi, feats + width :] = jnp.broadcast_to(raw, (step, LANES))
-        out_ref[lo:hi, feats : feats + width] = dot3(halves(scores), (vals[0][:hi], vals[1][:hi]), NN)
-
-
-def scan_kernel(backward, state_rows, mine_ref, got_ref, out_ref, norm_ref):
-    count = got_ref.shape[0]
-    mine = mine_ref[0]
+        numer = dot3(halves(scores), (vals[0][:hi], vals[1][:hi]), NN)
+        out_ref[lo:hi, feats : feats + width] = numer + dot3(fq, before, NT)
+
+
+def forward_scan_kernel(state_rows, place_ref, owner_ref, got_ref, blocks_ref, out_ref, norm_ref):
+    pairs = got_ref.shape[0]
+    mine = place_ref[0] // 2
+    odd = place_ref[0] % 2 == 1
     total = jnp.zeros((state_rows, LANES), jnp.float32)
-    norm = jnp.zeros((ROWS, LANES), jnp.float32)
-    for place in range(count - 1, -1, -1) if backward else range(count):
-        out_ref[place, :state_rows, :] = total
-        total = total + got_ref[place, :state_rows, :]
-        use = (place > mine) if backward else (place < mine)
-        tile = got_ref[place, state_rows : state_rows + ROWS, :]
-        norm = norm + jnp.where(use, tile, 0.0)
-    norm_ref[...] = norm
-
-
-def forward_scan_kernel(state_rows, mine_ref, owner_ref, got_ref, blocks_ref, out_ref, norm_ref):
-    scan_kernel(False, state_rows, mine_ref, got_ref, out_ref, norm_ref)
+    norm = jnp.zeros((NORM_ROWS, LANES), jnp.float32)
+    for pair in range(pairs):
+        out_ref[2 * pair, :state_rows, :] = total
+        out_ref[2 * pair + 1, :state_rows, :] = total
+        total = total + got_ref[pair, :state_rows, :]
+        even = got_ref[pair, state_rows : state_rows + NORM_ROWS, :]
+        last = got_ref[pair, state_rows + NORM_ROWS :, :]
+        use_even = (pair < mine) | ((pair == mine) & odd)
+        norm = norm + jnp.where(use_even, even, 0.0)
+        norm = norm + jnp.where(pair < mine, last, 0.0)
+    norm_ref[...] = jnp.concatenate([norm, jnp.zeros_like(norm)], axis=0)
     count, rows, width = blocks_ref.shape
     for place in range(count):
         owner = owner_ref[place]
@@ -119,8 +174,15 @@
             out_ref[owner, base : base + rows, :] = blocks_ref[place, :, c * LANES : (c + 1) * LANES]
 
 
-def backward_scan_kernel(state_rows, mine_ref, got_ref, term_ref, out_ref, norm_ref):
-    scan_kernel(True, state_rows, mine_ref, got_ref, out_ref, norm_ref)
+def backward_scan_kernel(state_rows, place_ref, got_ref, term_ref, out_ref, norm_ref):
+    mine = place_ref[0]
+    total = jnp.zeros((state_rows, LANES), jnp.float32)
+    norm = jnp.zeros((ROWS, LANES), jnp.float32)
+    for place in range(got_ref.shape[0] - 1, -1, -1):
+        out_ref[place, :state_rows, :] = total
+        total = total + got_ref[place, :state_rows, :]
+        norm = norm + jnp.where(place > mine, got_ref[place, state_rows:, :], 0.0)
+    norm_ref[...] = norm
     out_ref[:, state_rows:, :] = term_ref[...]
 
 
@@ -135,7 +197,7 @@
     count = got_ref.shape[0]
     chunks = feats // LANES
     state_rows = chunks * ROWS
-    state = unpack(got_ref, 0, chunks)
+    state = unpack_pairs(got_ref, chunks)
     for source in range(count):
         at = pl.multiple_of(within_ref[source] * block_rows, block_rows)
         for c in range(width // LANES):
@@ -168,7 +230,8 @@
 
 
 def weight_kernel(
-    queries, values, block_ref, feat_k, got_ref, norm_ref, grad_ref, term_ref, inner_ref, pre_ref
+    place_ref, queries, values, block_ref, feat_k, got_ref, norm_ref, grad_ref, low_ref, high_ref,
+    term_ref, inner_ref, pre_ref,
 ):
     tokens, feats = feat_k.shape
     width = values.shape[1]
@@ -177,7 +240,7 @@
     chunks = feats // LANES
     vals = halves(values[...])
     keys = halves(feat_k[...])
-    states = halves(unpack(got_ref, 0, chunks))
+    states = halves(unpack_pairs(got_ref, chunks) + even_state(place_ref, low_ref, high_ref))
     prev_norm = norm_row(norm_ref, chunks)
     for lo in range(0, tokens, step):
         hi = lo + step
@@ -229,6 +292,30 @@
     )(*args)
 
 
+def cut_kernel(in_ref, out_ref, sems):
+    heads, _, width = out_ref.shape
+    copies = [
+        pltpu.make_async_copy(in_ref.at[:, pl.ds(h * width, width)], out_ref.at[h], sems.at[h])
+        for h in range(heads)
+    ]
+    for copy in copies:
+        copy.start()
+    for copy in copies:
+        copy.wait()
+
+
+def cut_heads(rows, heads):
+    count, total = rows.shape
+    return pl.pallas_call(
+        cut_kernel,
+        out_shape=jax.ShapeDtypeStruct((heads, count, total // heads), rows.dtype),
+        in_specs=[pl.BlockSpec(memory_space=pl.ANY)],
+        out_specs=pl.BlockSpec(memory_space=pltpu.VMEM),
+        scratch_shapes=[pltpu.SemaphoreType.DMA((heads,))],
+        name="cut",
+    )(rows)
+
+
 def exchange(value, axis):
     return lax.all_to_all(value, axis, split_axis=0, concat_axis=0, tiled=True)
 
@@ -239,6 +326,7 @@
     feats = 2 * half
     count = lax.axis_size("seq")
     mine = lax.axis_index("seq")
+    heads = lax.axis_size("head")
     chunks = feats // LANES
     state_rows = chunks * ROWS
     block_rows = tokens // count
@@ -248,17 +336,25 @@
     slot_ids = lax.dynamic_index_in_dim(block_map, mine, 0, keepdims=False)
     owner_ids = slot_ids // count
     within = jnp.sum(jnp.where(block_map // count == mine, block_map % count, 0), axis=1).astype(jnp.int32)
-    gathered = lax.all_to_all(teacher_out, "head", split_axis=1, concat_axis=0, tiled=True)
+    gathered = exchange(cut_heads(teacher_out, heads), "head")
     blocks = gathered.reshape(count, block_rows, width)
 
-    feat_k, out1 = call(
-        key_kernel, [(tokens, feats), (count, state_rows + ROWS, LANES)], "vvv", 1.0,
-        (keys, key_map[0], values),
-    )
-    got1 = exchange(out1, "seq")
+    slices = count // 2
+    half_shape = (slices + 1, state_rows, LANES)
+    feat_k, send, keep = call(
+        key_kernel, [(tokens, feats), half_shape, half_shape], "svvv", 1.0,
+        (place, keys, key_map[0], values),
+    )
+    swapped = lax.ppermute(send, "seq", [(s, s ^ 1) for s in range(count)])
+    given = lax.ppermute(keep, "seq", [(s, s + 1) for s in range(0, count, 2)])
+    (out1,) = call(pair_kernel, [(slices, state_rows + ROWS, LANES)], "svv", 0.1, (place, keep, swapped))
+    parities = [list(range(p, count, 2)) for p in range(2)]
+    got1 = lax.all_to_all(
+        out1, "seq", split_axis=0, concat_axis=0, axis_index_groups=parities, tiled=True
+    )
     (block,) = call(
-        query_kernel, [(tokens, feats + width + LANES)], "vvvv", 2.0,
-        (queries, query_map[0], feat_k, values),
+        query_kernel, [(tokens, feats + width + LANES)], "svvvvvv", 2.0,
+        (place, queries, query_map[0], feat_k, values, given, swapped),
     )
     out2, prev_norm = call(
         functools.partial(forward_scan_kernel, state_rows),
@@ -273,8 +369,8 @@
     )
     got3 = exchange(out3, "seq")
     term_q, inner = call(
-        weight_kernel, [(count, term_rows, LANES), (tokens, feats)], "vvvvvvv", 4.0,
-        (queries, values, block, feat_k, got2, prev_norm, grads), [(tokens, half)],
+        weight_kernel, [(count, term_rows, LANES), (tokens, feats)], "svvvvvvvvv", 4.0,
+        (place, queries, values, block, feat_k, got2, prev_norm, grads, given, swapped), [(tokens, half)],
     )
     out4, next_norm = call(
         functools.partial(backward_scan_kernel, state_rows),

time: 172 us -> 194 us (1.13)
  starting transfers between devices: 30.9 us -> 41.6 us
  local copies, waits for them, and re-layouts: 11.1 us -> 17.1 us
  waiting for transfers between devices: 67.7 us -> 70 us
  Pallas kernels: 16.8 us -> 18.8 us
    ppermute x0 -> x2, waiting for transfers between devices: none -> 32.4 us  [the longest x1 27.9 us: per_device(): given = lax.ppermute(keep, 'seq', [(s, s + 1) for s in range(0, count, 2)])]
    all_to_all x3, waiting for transfers between devices: 54.8 us -> 26.1 us  [exchange(): return lax.all_to_all(value, axis, split_axis=0, concat_axis=0, tiled=True)]
    ppermute x0 -> x2, starting transfers between devices: none -> 8.2 us  [the longest x1 6.91 us: per_device(): swapped = lax.ppermute(send, 'seq', [(s, s ^ 1) for s in range(count)])]
    unnamed x34 -> x46, local copies, waits for them, and re-layouts: 9.11 us -> 17.1 us
    all_to_all x1, starting transfers between devices: 7.21 us -> 10.8 us  [per_device(): lax.all_to_all(out1, 'seq', split_axis=0, concat_axis=0, axis_index_group...]
    all_to_all x1 -> x0, local copies, waits for them, and re-layouts: 2.01 us -> none  [per_device(): lax.all_to_all(teacher_out, 'head', split_axis=1, concat_axis=0, tiled=True)]
    pallas_call x0 -> x1, Pallas kernels: none -> 1.94 us  [cut_heads(): pl.pallas_call(cut_kernel, out_shape=jax.ShapeDtypeStruct((heads, count,...]
    pallas_call x8 -> x9, Pallas kernels: 16.8 us -> 16.8 us  [call(): pl.pallas_call(body, out_shape=[jax.ShapeDtypeStruct(shape, jnp.float32)...]
  transfers between devices with their start and end apart: 4 -> 6, of which waited for: 4 -> 5; matrix products, arithmetic and copies ran while one was open for 1% -> 0% of each run, Pallas kernels for 5% -> 4%
where the time goes in v4:
time: 194 us; the launch traced here: 193 us
  waiting for transfers between devices  70 us (36%)
  blocking collectives  44.1 us (23%)
  starting transfers between devices  41.6 us (21%)
  Pallas kernels  18.8 us (10%)
  local copies, waits for them, and re-layouts  17.1 us (9%)
    all_to_all x2, blocking collectives, exchange(): return lax.all_to_all(value, axis, split_axis=0, concat_axis=0, tiled=True)  44.1 us
    ppermute x1, waiting for transfers between devices, per_device(): given = lax.ppermute(keep, 'seq', [(s, s + 1) for s in range(0, count, 2)])  27.9 us
    all_to_all x3, waiting for transfers between devices, exchange(): return lax.all_to_all(value, axis, split_axis=0, concat_axis=0, tiled=True)  26.1 us
    all_to_all x3, starting transfers between devices, exchange(): return lax.all_to_all(value, axis, split_axis=0, concat_axis=0, tiled=True)  22.6 us
    unnamed x46, local copies, waits for them, and re-layouts  17.1 us
    pallas_call x9, Pallas kernels, call(): pl.pallas_call(body, out_shape=[jax.ShapeDtypeStruct(shape, jnp.float32)...  16.8 us
    all_to_all x1, waiting for transfers between devices, per_device(): lax.all_to_all(out1, 'seq', split_axis=0, concat_axis=0, axis_index_group...  11.6 us
    all_to_all x1, starting transfers between devices, per_device(): lax.all_to_all(out1, 'seq', split_axis=0, concat_axis=0, axis_index_group...  10.8 us
  transfers between devices with their start and end apart: 6, of which 5 were waited for; matrix products, arithmetic and copies ran while one was open for 0% of the time, Pallas kernels for 4%

profile of v4, /device:TPU:64, one launch (start us, length us, event | category | flops | bytes accessed | tf_op | source)
XLA Modules:
  0.0 192.6 jit_solution(16039971064101615814)
XLA Ops:
  0.6 0.0 copy-start.2
  0.6 1.0 copy-done.2
  1.7 1.0 copy-done.4
  2.7 0.9 copy-done.13
  3.7 2.2 %shard_map.86 = (f32[512,512]{1,0:T(8,128)S(1)}, f32[17,32,128]{2,1,0:T(8,128)S(1)}, f32[17,32,128]{2,1,0:T(8,128)S(1)}) custom-call(s32[1]{0:T(128)} %bitcast.place_ref, f32[512,256]{1,0:T(8,128)S(1)} %copy-done.2, f32[256,256]{1,0:T(8,128)S(1)} %bitcast.15, f32[512,256]{1,0:T(8,128)S(1)} %copy-done.4), custom_call_target="tpu_custom_call" | custom-call | flops 1000000000 | bytes 1048576 | tf_op jit(solution)/shard_map/pallas_call | solution.py:284
  5.8 0.0 copy-start.22
  5.9 6.9 %collective-permute-start.1 = (f32[17,32,128]{2,1,0:T(8,128)S(1)}, f32[17,32,128]{2,1,0:T(8,128)S(1)}, u32[]{:S(2)}, u32[]{:S(2)}) collective-permute-start(f32[17,32,128]{2,1,0:T(8,128)S(1)} %get-tuple-element.17), channel_id=1, source_target_pairs={{0,16},{16,0},{32,48},{48,32},{64,80},{80,64},{96,112},{112,96},{1... | collective-permute-start | bytes 835592 | tf_op jit(solution)/shard_map/ppermute | solution.py:348
  12.8 4.5 %collective-permute-done.1.high_ref.got_ref = f32[17,32,128]{2,1,0:T(8,128)S(1)} collective-permute-done((f32[17,32,128]{2,1,0:T(8,128)S(1)}, f32[17,32,128]{2,1,0:T(8,128)S(1)}, u32[]{:S(2)}, u32[]{:S(2)}) %collective-permute-start.1) | collective-permute-done | bytes 278560 | tf_op jit(solution)/shard_map/ppermute | solution.py:348
  17.3 0.8 shard_map.88
  18.0 10.8 %all-to-all-start = ((f32[16,40,128]{2,1,0:T(8,128)}), f32[16,40,128]{2,1,0:T(8,128)S(1)}, u32[]{:S(2)}, u32[]{:S(2)}) async-start(f32[16,40,128]{2,1,0:T(8,128)} %shard_map.88), calls=%async_computation | async-start | bytes 655360 | tf_op jit(solution)/shard_map/all_to_all | solution.py:352
  28.9 1.9 %cut.1 = f32[16,32,256]{2,1,0:T(8,128)} custom-call(f32[32,4096]{1,0:T(8,128)} %in_ref.1), custom_call_target="tpu_custom_call" | custom-call | tf_op jit(solution)/shard_map/cut/pallas_call | solution.py:309
  30.8 0.0 copy-start.5
  30.9 0.0 copy-start.14
  30.9 11.6 %all-to-all-done.got_ref = f32[16,40,128]{2,1,0:T(8,128)S(1)} async-done(((f32[16,40,128]{2,1,0:T(8,128)}), f32[16,40,128]{2,1,0:T(8,128)S(1)}, u32[]{:S(2)}, u32[]{:S(2)}) %all-to-all-start) | async-done | bytes 327712 | tf_op jit(solution)/shard_map/all_to_all | solution.py:352
  42.5 7.2 %all-to-all-start.1 = ((f32[16,32,256]{2,1,0:T(8,128)}), f32[16,32,256]{2,1,0:T(8,128)S(1)}, u32[]{:S(2)}, u32[]{:S(2)}) async-start(f32[16,32,256]{2,1,0:T(8,128)} %cut.1), calls=%async_computation.1 | async-start | bytes 1048576 | tf_op jit(solution)/shard_map/all_to_all | solution.py:320
  49.7 15.9 %all-to-all-done.1 = f32[16,32,256]{2,1,0:T(8,128)S(1)} async-done(((f32[16,32,256]{2,1,0:T(8,128)}), f32[16,32,256]{2,1,0:T(8,128)S(1)}, u32[]{:S(2)}, u32[]{:S(2)}) %all-to-all-start.1) | async-done | bytes 524320 | tf_op jit(solution)/shard_map/all_to_all | solution.py:320
  65.6 1.6 shard_map.89
  67.2 4.3 %all-to-all-start.2 = ((f32[32,64,128]{2,1,0:T(8,128)}), f32[32,64,128]{2,1,0:T(8,128)S(1)}, u32[]{:S(2)}, u32[]{:S(2)}) async-start(f32[32,64,128]{2,1,0:T(8,128)} %get-tuple-element.18), calls=%async_computation.2 | async-start | bytes 2097152 | tf_op jit(solution)/shard_map/all_to_all | solution.py:320
  71.5 1.3 collective-permute-start
  72.8 0.1 fusion.2.within_ref
  72.9 27.9 %collective-permute-done.low_ref = f32[17,32,128]{2,1,0:T(8,128)S(1)} collective-permute-done((f32[17,32,128]{2,1,0:T(8,128)S(1)}, f32[17,32,128]{2,1,0:T(8,128)S(1)}, u32[]{:S(2)}, u32[]{:S(2)}) %collective-permute-start) | collective-permute-done | bytes 278560 | tf_op jit(solution)/shard_map/ppermute | solution.py:349
  100.8 0.0 copy-done.5
  100.8 1.0 copy-done.9
  101.8 3.1 %shard_map.87.block_ref = f32[512,896]{1,0:T(8,128)S(1)} custom-call(s32[1]{0:T(128)} %bitcast.place_ref, f32[512,256]{1,0:T(8,128)S(1)} %copy-done.9, f32[256,256]{1,0:T(8,128)S(1)} %bitcast.16, f32[512,512]{1,0:T(8,128)S(1)} %get-tuple-element.15.feat_k, f32[512,256]{1,0:T(8,128)S(1)} %copy-done.5, f32[17,32,128]{2,1,0:T(8,128)S(1)} %collective-permute-done.low_ref, ...), custom_call_target="tpu_custom_call" | custom-call | flops 2000000000 | bytes 1048576 | tf_op jit(solution)/shard_map/pallas_call | solution.py:284
  104.9 0.0 copy-start.11
  104.9 0.7 copy-done.11
  105.7 1.2 copy-done.17
  106.9 0.0 all-to-all-done.2.got_ref
  106.9 0.0 copy-done.15
  106.9 1.9 copy-done.18
  108.8 3.4 %shard_map.90 = (f32[512,384]{1,0:T(8,128)S(1)}, f32[32,40,128]{2,1,0:T(8,128)}) custom-call(s32[32]{0:T(128)S(1)} %fusion.2.within_ref, f32[32,64,128]{2,1,0:T(8,128)S(1)} %all-to-all-done.2.got_ref, f32[8,128]{1,0:T(8,128)S(1)} %get-tuple-element.19.norm_ref, f32[512,896]{1,0:T(8,128)S(1)} %copy-done.18), custom_call_target="tpu_custom_call" | custom-call | flops 1000000000 | bytes 1048576 | tf_op jit(solution)/shard_map/pallas_call | solution.py:284
  112.2 0.9 copy-done.20
  113.1 11.1 %all-to-all-start.3 = ((f32[32,40,128]{2,1,0:T(8,128)}), f32[32,40,128]{2,1,0:T(8,128)S(1)}, u32[]{:S(2)}, u32[]{:S(2)}) async-start(f32[32,40,128]{2,1,0:T(8,128)} %get-tuple-element.22), calls=%async_computation.3 | async-start | bytes 1310720 | tf_op jit(solution)/shard_map/all_to_all | solution.py:320
  124.2 1.2 copy-done.1
  125.4 1.0 copy-done.10
  126.5 1.0 copy-done.12
  127.4 0.7 copy-done.16
  128.1 1.5 copy-done.19
  129.6 1.1 copy-done.21
  130.8 3.2 %shard_map.91 = (f32[32,16,128]{2,1,0:T(8,128)S(1)}, f32[512,512]{1,0:T(8,128)S(1)}) custom-call(s32[1]{0:T(128)} %bitcast.place_ref, f32[512,256]{1,0:T(8,128)S(1)} %copy-done.10, f32[512,256]{1,0:T(8,128)S(1)} %copy-done.5, f32[512,896]{1,0:T(8,128)S(1)} %copy-done.19, f32[512,512]{1,0:T(8,128)S(1)} %get-tuple-element.15.feat_k, ...), custom_call_target="tpu_custom_call" | custom-call | flops 4000000000 | bytes 1048576 | tf_op jit(solution)/shard_map/pallas_call | solution.py:284
  133.9 0.7 copy-done.7
  134.6 10.2 %all-to-all-done.3.got_ref = f32[32,40,128]{2,1,0:T(8,128)S(1)} async-done(((f32[32,40,128]{2,1,0:T(8,128)}), f32[32,40,128]{2,1,0:T(8,128)S(1)}, u32[]{:S(2)}, u32[]{:S(2)}) %all-to-all-start.3) | async-done | bytes 655392 | tf_op jit(solution)/shard_map/all_to_all | solution.py:320
  144.8 1.0 copy-done.8
  145.8 0.1 shard_map.92
  145.9 27.7 %all_to_all.30.got_ref = f32[32,48,128]{2,1,0:T(8,128)S(1)} all-to-all(f32[32,48,128]{2,1,0:T(8,128)S(1)} %get-tuple-element.24), channel_id=1, replica_groups=mesh['seq'=32,'head'=16] {'seq'}, dimensions={0} | all-to-all | bytes 1572864 | tf_op jit(solution)/shard_map/all_to_all | solution.py:320
  173.5 1.9 %shard_map.93 = (f32[32,16,128]{2,1,0:T(8,128)S(1)}, f32[8,256]{1,0:T(8,128)}) custom-call(f32[512,256]{1,0:T(8,128)S(1)} %copy-done.3, f32[512,256]{1,0:T(8,128)S(1)} %copy-done.6, f32[512,512]{1,0:T(8,128)S(1)} %get-tuple-element.15.feat_k, f32[512,512]{1,0:T(8,128)S(1)} %get-tuple-element.21.inner, f32[32,48,128]{2,1,0:T(8,128)S(1)} %all_to_all.30.got_ref, ...), custom_call_target="tpu_custom_call" | custom-call | flops 1000000000 | bytes 1048576 | tf_op jit(solution)/shard_map/pallas_call | solution.py:284
  175.5 16.5 %all_to_all.31.got_ref = f32[32,16,128]{2,1,0:T(8,128)S(1)} all-to-all(f32[32,16,128]{2,1,0:T(8,128)S(1)} %get-tuple-element.27), channel_id=1, replica_groups=mesh['seq'=32,'head'=16] {'seq'}, dimensions={0} | all-to-all | bytes 524288 | tf_op jit(solution)/shard_map/all_to_all | solution.py:320
  191.9 0.6 shard_map.94
  (24 shorter events, 0.1 us)
Async XLA Ops:
  0.6 1.0 copy-start.2
  1.7 1.0 copy-start.4
  2.7 0.9 copy-start.13
  5.8 43.8 %copy-start.22 = (s32[32,32]{1,0:T(8,128)S(1)}, s32[32,32]{1,0:T(8,128)}, u32[]{:S(2)}) copy-start(s32[32,32]{1,0:T(8,128)} %param.13) | copy-start | bytes 12292
  5.9 11.4 %collective-permute-start.1 = (f32[17,32,128]{2,1,0:T(8,128)S(1)}, f32[17,32,128]{2,1,0:T(8,128)S(1)}, u32[]{:S(2)}, u32[]{:S(2)}) collective-permute-start(f32[17,32,128]{2,1,0:T(8,128)S(1)} %get-tuple-element.17), channel_id=1, source_target_pairs={{0,16},{16,0},{32,48},{48,32},{64,80},{80,64},{96,112},{112,96},{1... | collective-permute-start | bytes 835592 | tf_op jit(solution)/shard_map/ppermute | solution.py:348
  18.0 24.4 %all-to-all-start = ((f32[16,40,128]{2,1,0:T(8,128)}), f32[16,40,128]{2,1,0:T(8,128)S(1)}, u32[]{:S(2)}, u32[]{:S(2)}) async-start(f32[16,40,128]{2,1,0:T(8,128)} %shard_map.88), calls=%async_computation | async-start | bytes 655360 | tf_op jit(solution)/shard_map/all_to_all | solution.py:352
  30.8 69.9 %copy-start.5 = (f32[512,256]{1,0:T(8,128)S(1)}, f32[512,256]{1,0:T(8,128)}, u32[]{:S(2)}) copy-start(f32[512,256]{1,0:T(8,128)} %values.7) | copy-start | bytes 1572868
  30.9 69.9 %copy-start.14 = (f32[1,256,256]{2,1,0:T(8,128)S(1)}, f32[1,256,256]{2,1,0:T(8,128)}, u32[]{:S(2)}) copy-start(f32[1,256,256]{2,1,0:T(8,128)} %param.11) | copy-start | bytes 786436
  42.5 23.1 %all-to-all-start.1 = ((f32[16,32,256]{2,1,0:T(8,128)}), f32[16,32,256]{2,1,0:T(8,128)S(1)}, u32[]{:S(2)}, u32[]{:S(2)}) async-start(f32[16,32,256]{2,1,0:T(8,128)} %cut.1), calls=%async_computation.1 | async-start | bytes 1048576 | tf_op jit(solution)/shard_map/all_to_all | solution.py:320
  67.2 39.7 %copy-start.15 = (f32[8,128]{1,0:T(8,128)}, f32[8,128]{1,0:T(8,128)S(1)}, u32[]{:S(2)}) copy-start(f32[8,128]{1,0:T(8,128)S(1)} %get-tuple-element.19.norm_ref) | copy-start | bytes 12292
  67.2 39.7 %all-to-all-start.2 = ((f32[32,64,128]{2,1,0:T(8,128)}), f32[32,64,128]{2,1,0:T(8,128)S(1)}, u32[]{:S(2)}, u32[]{:S(2)}) async-start(f32[32,64,128]{2,1,0:T(8,128)} %get-tuple-element.18), calls=%async_computation.2 | async-start | bytes 2097152 | tf_op jit(solution)/shard_map/all_to_all | solution.py:320
  71.5 29.3 %collective-permute-start = (f32[17,32,128]{2,1,0:T(8,128)S(1)}, f32[17,32,128]{2,1,0:T(8,128)S(1)}, u32[]{:S(2)}, u32[]{:S(2)}) collective-permute-start(f32[17,32,128]{2,1,0:T(8,128)S(1)} %get-tuple-element.16.keep_ref), channel_id=1, source_target_pairs={{0,16},{32,48},{64,80},{96,112},{128,144},{160,176},{192,208},{224... | collective-permute-start | bytes 835592 | tf_op jit(solution)/shard_map/ppermute | solution.py:349
  100.8 1.0 copy-start.9
  104.9 0.7 copy-start.11
  105.7 1.2 copy-start.17
  106.9 5.2 %copy-start = (f32[32,64,128]{2,1,0:T(8,128)}, f32[32,64,128]{2,1,0:T(8,128)S(1)}, u32[]{:S(2)}) copy-start(f32[32,64,128]{2,1,0:T(8,128)S(1)} %all-to-all-done.2.got_ref) | copy-start | bytes 3145732
  106.9 1.9 copy-start.18
  112.2 0.9 copy-start.20
  113.1 31.7 %all-to-all-start.3 = ((f32[32,40,128]{2,1,0:T(8,128)}), f32[32,40,128]{2,1,0:T(8,128)S(1)}, u32[]{:S(2)}, u32[]{:S(2)}) async-start(f32[32,40,128]{2,1,0:T(8,128)} %get-tuple-element.22), calls=%async_computation.3 | async-start | bytes 1310720 | tf_op jit(solution)/shard_map/all_to_all | solution.py:320
  124.2 1.2 copy-start.1
  125.4 1.0 copy-start.10
  126.5 1.0 copy-start.12
  127.4 0.7 copy-start.16
  128.1 1.5 copy-start.19
  129.6 1.1 copy-start.21
  133.9 0.7 copy-start.7
  134.6 38.9 %copy-start.3 = (f32[512,256]{1,0:T(8,128)S(1)}, f32[512,256]{1,0:T(8,128)}, u32[]{:S(2)}) copy-start(f32[512,256]{1,0:T(8,128)} %keys.3) | copy-start | bytes 1572868
  144.8 28.7 %copy-start.6 = (f32[512,256]{1,0:T(8,128)S(1)}, f32[512,256]{1,0:T(8,128)}, u32[]{:S(2)}) copy-start(f32[512,256]{1,0:T(8,128)} %values.7) | copy-start | bytes 1572868
  144.8 1.0 copy-start.8

commit v5 on v4

--- a/solution.py
+++ b/solution.py
@@ -150,7 +150,17 @@
         out_ref[lo:hi, feats : feats + width] = numer + dot3(fq, before, NT)
 
 
-def forward_scan_kernel(state_rows, place_ref, owner_ref, got_ref, blocks_ref, out_ref, norm_ref):
+def owner_kernel(owner_ref, blocks_ref, out_ref):
+    count, rows, width = blocks_ref.shape
+    for place in range(count):
+        owner = owner_ref[place]
+        for c in range(width // LANES):
+            out_ref[owner, c * rows : (c + 1) * rows, :] = blocks_ref[place, :, c * LANES : (c + 1) * LANES]
+
+
+def forward_scan_kernel(state_rows, place_ref, got_ref, rest_ref, out_ref, norm_ref, sem):
+    rest = pltpu.make_async_copy(rest_ref, out_ref.at[:, state_rows:, :], sem)
+    rest.start()
     pairs = got_ref.shape[0]
     mine = place_ref[0] // 2
     odd = place_ref[0] % 2 == 1
@@ -166,15 +176,12 @@
         norm = norm + jnp.where(use_even, even, 0.0)
         norm = norm + jnp.where(pair < mine, last, 0.0)
     norm_ref[...] = jnp.concatenate([norm, jnp.zeros_like(norm)], axis=0)
-    count, rows, width = blocks_ref.shape
-    for place in range(count):
-        owner = owner_ref[place]
-        for c in range(width // LANES):
-            base = state_rows + c * rows
-            out_ref[owner, base : base + rows, :] = blocks_ref[place, :, c * LANES : (c + 1) * LANES]
-
-
-def backward_scan_kernel(state_rows, place_ref, got_ref, term_ref, out_ref, norm_ref):
+    rest.wait()
+
+
+def backward_scan_kernel(state_rows, place_ref, got_ref, rest_ref, out_ref, norm_ref, sem):
+    rest = pltpu.make_async_copy(rest_ref, out_ref.at[:, state_rows:, :], sem)
+    rest.start()
     mine = place_ref[0]
     total = jnp.zeros((state_rows, LANES), jnp.float32)
     norm = jnp.zeros((ROWS, LANES), jnp.float32)
@@ -183,7 +190,7 @@
         total = total + got_ref[place, :state_rows, :]
         norm = norm + jnp.where(place > mine, got_ref[place, state_rows:, :], 0.0)
     norm_ref[...] = norm
-    out_ref[:, state_rows:, :] = term_ref[...]
+    rest.wait()
 
 
 def norm_row(norm_ref, count):
@@ -191,8 +198,11 @@
 
 
 def middle_kernel(
-    block_rows, feats, within_ref, got_ref, norm_ref, block_ref, grad_ref, out_ref, teacher_ref
+    block_rows, feats, within_ref, got_ref, norm_ref, block_hbm, grad_hbm, out_ref,
+    teacher_ref, block_ref, grad_ref, sems,
 ):
+    fetch = pltpu.make_async_copy(block_hbm, block_ref, sems.at[0])
+    fetch.start()
     width = teacher_ref.shape[1]
     count = got_ref.shape[0]
     chunks = feats // LANES
@@ -205,9 +215,11 @@
             teacher_ref[pl.ds(at, block_rows), c * LANES : (c + 1) * LANES] = got_ref[
                 source, base : base + block_rows, :
             ]
+    state = halves(state)
+    fetch.wait()
     fq = block_ref[:, :feats]
     fq_pair = halves(fq)
-    numerator = block_ref[:, feats : feats + width] + dot3(fq_pair, halves(state), NT)
+    numerator = block_ref[:, feats : feats + width] + dot3(fq_pair, state, NT)
     prev_norm = norm_row(norm_ref, chunks)
     raw_sum = block_ref[:, feats + width : feats + width + 1] + jnp.sum(fq * prev_norm, axis=-1, keepdims=True)
     divisor = jnp.maximum(raw_sum, 1.0)
@@ -217,8 +229,11 @@
     grad_div = jnp.where(raw_sum > 1.0, -jnp.sum(mismatch * student, axis=-1, keepdims=True) / divisor, 0.0)
     grad_ref[:, :width] = grad_num
     grad_ref[:, width:] = jnp.broadcast_to(grad_div, (grad_div.shape[0], LANES))
+    store = pltpu.make_async_copy(grad_ref, grad_hbm.at[0], sems.at[1])
+    store.start()
     pack(out_ref, 0, dot3(halves(grad_num), fq_pair, TN))
     pack_norm(out_ref, state_rows, jnp.sum(grad_div * fq, axis=0, keepdims=True))
+    store.wait()
 
 
 def back_pair(feat, grad, half):
@@ -262,14 +277,24 @@
     pack(term_ref, 0, dot3(halves(queries[...]), halves(pre_ref[...]), TN))
 
 
-def close_kernel(keys, values, feat_k, inner, got_ref, norm_ref, term_ref, query_ref):
+def close_kernel(
+    keys_hbm, values, feat_hbm, inner_hbm, got_ref, norm_ref, term_ref, query_ref, keys, feat_k, inner, sems
+):
+    pairs = ((inner_hbm, inner), (feat_hbm, feat_k), (keys_hbm, keys))
+    fetches = [pltpu.make_async_copy(src, dst, sems.at[i]) for i, (src, dst) in enumerate(pairs)]
+    for fetch in fetches:
+        fetch.start()
     feats = feat_k.shape[1]
     chunks = feats // LANES
     state = unpack(got_ref, 0, chunks)
-    grad_fk = inner[...] + dot3(halves(values[...]), halves(state), NN) + norm_row(norm_ref, chunks)
+    grad_fk = dot3(halves(values[...]), halves(state), NN) + norm_row(norm_ref, chunks)
+    sum_kernel(chunks * ROWS, got_ref, query_ref)
+    fetches[0].wait()
+    grad_fk = grad_fk + inner[...]
+    fetches[1].wait()
     grad_pk = back_pair(feat_k[...], grad_fk, feats // 2)
+    fetches[2].wait()
     pack(term_ref, 0, dot3(halves(keys[...]), halves(grad_pk), TN))
-    sum_kernel(chunks * ROWS, got_ref, query_ref)
 
 
 def sum_kernel(base, got_ref, out_ref):
@@ -278,16 +303,16 @@
         out_ref[:, c * LANES : (c + 1) * LANES] = jnp.sum(part, axis=0)
 
 
-def call(body, outs, spaces, cost, args, scratch=()):
-    vmem = pl.BlockSpec(memory_space=pltpu.VMEM)
-    smem = pl.BlockSpec(memory_space=pltpu.SMEM)
+def call(body, outs, spaces, cost, args, scratch=(), sems=0, out_spaces=None, grant=24000):
+    kinds = {"v": pltpu.VMEM, "s": pltpu.SMEM, "h": pltpu.HBM}
     return pl.pallas_call(
         body,
         out_shape=[jax.ShapeDtypeStruct(shape, jnp.float32) for shape in outs],
-        in_specs=[smem if kind == "s" else vmem for kind in spaces],
-        out_specs=[vmem] * len(outs),
-        scratch_shapes=[pltpu.VMEM(shape, jnp.float32) for shape in scratch],
-        compiler_params=pltpu.CompilerParams(vmem_limit_bytes=24 * 1024 * 1024),
+        in_specs=[pl.BlockSpec(memory_space=kinds[kind]) for kind in spaces],
+        out_specs=[pl.BlockSpec(memory_space=kinds[kind]) for kind in out_spaces or "v" * len(outs)],
+        scratch_shapes=[pltpu.VMEM(shape, jnp.float32) for shape in scratch]
+        + ([pltpu.SemaphoreType.DMA((sems,))] if sems > 1 else [pltpu.SemaphoreType.DMA] * sems),
+        compiler_params=pltpu.CompilerParams(vmem_limit_bytes=grant * 1024),
         cost_estimate=pl.CostEstimate(flops=int(cost * 1e9), bytes_accessed=1 << 20, transcendentals=0),
     )(*args)
 
@@ -356,18 +381,22 @@
         query_kernel, [(tokens, feats + width + LANES)], "svvvvvv", 2.0,
         (place, queries, query_map[0], feat_k, values, given, swapped),
     )
+    teacher_rows = block_rows * (width // LANES)
+    (placed,) = call(owner_kernel, [(count, teacher_rows, LANES)], "sv", 1.0, (owner_ids, blocks))
     out2, prev_norm = call(
         functools.partial(forward_scan_kernel, state_rows),
-        [(count, state_rows + block_rows * (width // LANES), LANES), (ROWS, LANES)],
-        "ssvv", 0.1, (place, owner_ids, got1, blocks),
+        [(count, state_rows + teacher_rows, LANES), (ROWS, LANES)],
+        "svh", 0.1, (place, got1, placed), sems=1, grant=54500,
     )
     got2 = exchange(out2, "seq")
     grads, out3 = call(
         functools.partial(middle_kernel, block_rows, feats),
-        [(tokens, width + LANES), (count, state_rows + ROWS, LANES)],
-        "svvv", 1.0, (within, got2, prev_norm, block), [(tokens, width)],
+        [(3, tokens, width + LANES), (count, state_rows + ROWS, LANES)],
+        "svvh", 1.0, (within, got2, prev_norm, block),
+        [(tokens, width), (tokens, feats + width + LANES), (tokens, width + LANES)], 2, "hv", 52000,
     )
     got3 = exchange(out3, "seq")
+    grads = grads[0]
     term_q, inner = call(
         weight_kernel, [(count, term_rows, LANES), (tokens, feats)], "svvvvvvvvv", 4.0,
         (place, queries, values, block, feat_k, got2, prev_norm, grads, given, swapped), [(tokens, half)],
@@ -375,12 +404,13 @@
     out4, next_norm = call(
         functools.partial(backward_scan_kernel, state_rows),
         [(count, state_rows + term_rows, LANES), (ROWS, LANES)],
-        "svv", 0.1, (place, got3, term_q),
+        "svh", 0.1, (place, got3, term_q), sems=1, grant=54500,
     )
     got4 = exchange(out4, "seq")
     out5, grad_query = call(
-        close_kernel, [(count, term_rows, LANES), (width // count, half)], "vvvvvv", 1.0,
+        close_kernel, [(count, term_rows, LANES), (width // count, half)], "hvhhvv", 1.0,
         (keys, values, feat_k, inner, got4, next_norm),
+        [(tokens, width), (tokens, feats), (tokens, feats)], 3, grant=54500,
     )
     got5 = exchange(out5, "seq")
     (grad_key,) = call(functools.partial(sum_kernel, 0), [(width // count, half)], "v", 0.1, (got5,))

time: 194 us -> 184 us (0.948)
  waiting for transfers between devices: 70 us -> 61.6 us
  Pallas kernels: 18.8 us -> 26.1 us
  local copies, waits for them, and re-layouts: 17.1 us -> 12.5 us
  starting transfers between devices: 41.6 us -> 37.9 us
    all_to_all x3, waiting for transfers between devices: 26.1 us -> 12.3 us  [exchange(): return lax.all_to_all(value, axis, split_axis=0, concat_axis=0, tiled=True)]
    pallas_call x9 -> x10, Pallas kernels: 16.8 us -> 24.2 us  [call(): pl.pallas_call(body, out_shape=[jax.ShapeDtypeStruct(shape, jnp.float32)...]
    unnamed x46 -> x30, local copies, waits for them, and re-layouts: 17.1 us -> 11.3 us
    ppermute x1, starting transfers between devices: 6.91 us -> 3.27 us  [per_device(): swapped = lax.ppermute(send, 'seq', [(s, s ^ 1) for s in range(count)])]
    ppermute x1, waiting for transfers between devices: 4.51 us -> 7.58 us  [per_device(): swapped = lax.ppermute(send, 'seq', [(s, s ^ 1) for s in range(count)])]
    all_to_all x1, waiting for transfers between devices: 11.6 us -> 13.9 us  [per_device(): lax.all_to_all(out1, 'seq', split_axis=0, concat_axis=0, axis_index_group...]
  transfers between devices with their start and end apart: 6 -> 6, of which waited for: 5 -> 4; matrix products, arithmetic and copies ran while one was open for 0% -> 1% of each run, Pallas kernels for 4% -> 5%
where the time goes in v5:
time: 184 us; the launch traced here: 183 us
  waiting for transfers between devices  61.6 us (33%)
  blocking collectives  43.9 us (24%)
  starting transfers between devices  37.9 us (21%)
  Pallas kernels  26.1 us (14%)
  local copies, waits for them, and re-layouts  12.5 us (7%)
    all_to_all x2, blocking collectives, exchange(): return lax.all_to_all(value, axis, split_axis=0, concat_axis=0, tiled=True)  43.9 us
    ppermute x1, waiting for transfers between devices, per_device(): given = lax.ppermute(keep, 'seq', [(s, s + 1) for s in range(0, count, 2)])  27.9 us
    pallas_call x10, Pallas kernels, call(): pl.pallas_call(body, out_shape=[jax.ShapeDtypeStruct(shape, jnp.float32)...  24.2 us
    all_to_all x3, starting transfers between devices, exchange(): return lax.all_to_all(value, axis, split_axis=0, concat_axis=0, tiled=True)  21.4 us
    all_to_all x1, waiting for transfers between devices, per_device(): lax.all_to_all(out1, 'seq', split_axis=0, concat_axis=0, axis_index_group...  13.9 us
    all_to_all x3, waiting for transfers between devices, exchange(): return lax.all_to_all(value, axis, split_axis=0, concat_axis=0, tiled=True)  12.3 us
    all_to_all x1, starting transfers between devices, per_device(): lax.all_to_all(out1, 'seq', split_axis=0, concat_axis=0, axis_index_group...  12 us
    unnamed x30, local copies, waits for them, and re-layouts  11.3 us
  transfers between devices with their start and end apart: 6, of which 4 were waited for; matrix products, arithmetic and copies ran while one was open for 1% of the time, Pallas kernels for 5%

profile of v5, /device:TPU:64, one launch (start us, length us, event | category | flops | bytes accessed | tf_op | source)
XLA Modules:
  0.0 183.0 jit_solution(3074849654550216197)
XLA Ops:
  0.6 2.0 %cut.1 = f32[16,32,256]{2,1,0:T(8,128)} custom-call(f32[32,4096]{1,0:T(8,128)} %in_ref.1), custom_call_target="tpu_custom_call" | custom-call | tf_op jit(solution)/shard_map/cut/pallas_call | solution.py:334
  2.6 7.2 %all-to-all-start.1 = ((f32[16,32,256]{2,1,0:T(8,128)}), f32[16,32,256]{2,1,0:T(8,128)S(1)}, u32[]{:S(2)}, u32[]{:S(2)}) async-start(f32[16,32,256]{2,1,0:T(8,128)} %cut.1), calls=%async_computation.1 | async-start | bytes 1048576 | tf_op jit(solution)/shard_map/all_to_all | solution.py:345
  9.8 0.0 copy-start.2
  9.8 1.0 copy-done.2
  10.9 1.0 copy-done.3
  11.9 0.9 copy-done.10
  12.9 2.2 %shard_map.86 = (f32[512,512]{1,0:T(8,128)S(1)}, f32[17,32,128]{2,1,0:T(8,128)S(1)}, f32[17,32,128]{2,1,0:T(8,128)S(1)}) custom-call(s32[1]{0:T(128)} %bitcast.place_ref, f32[512,256]{1,0:T(8,128)S(1)} %copy-done.2, f32[256,256]{1,0:T(8,128)S(1)} %bitcast.17, f32[512,256]{1,0:T(8,128)S(1)} %copy-done.3), custom_call_target="tpu_custom_call" | custom-call | flops 1000000000 | bytes 1048576 | tf_op jit(solution)/shard_map/pallas_call | solution.py:308
  15.0 0.0 copy-start
  15.0 3.3 %collective-permute-start.1 = (f32[17,32,128]{2,1,0:T(8,128)S(1)}, f32[17,32,128]{2,1,0:T(8,128)S(1)}, u32[]{:S(2)}, u32[]{:S(2)}) collective-permute-start(f32[17,32,128]{2,1,0:T(8,128)S(1)} %get-tuple-element.17), channel_id=1, source_target_pairs={{0,16},{16,0},{32,48},{48,32},{64,80},{80,64},{96,112},{112,96},{1... | collective-permute-start | bytes 835592 | tf_op jit(solution)/shard_map/ppermute | solution.py:373
  18.3 7.6 %collective-permute-done.1.high_ref.got_ref = f32[17,32,128]{2,1,0:T(8,128)S(1)} collective-permute-done((f32[17,32,128]{2,1,0:T(8,128)S(1)}, f32[17,32,128]{2,1,0:T(8,128)S(1)}, u32[]{:S(2)}, u32[]{:S(2)}) %collective-permute-start.1) | collective-permute-done | bytes 278560 | tf_op jit(solution)/shard_map/ppermute | solution.py:373
  25.9 0.8 shard_map.88
  26.7 0.0 all-to-all-done.1
  26.7 12.0 %all-to-all-start = ((f32[16,40,128]{2,1,0:T(8,128)}), f32[16,40,128]{2,1,0:T(8,128)S(1)}, u32[]{:S(2)}, u32[]{:S(2)}) async-start(f32[16,40,128]{2,1,0:T(8,128)} %shard_map.88), calls=%async_computation | async-start | bytes 655360 | tf_op jit(solution)/shard_map/all_to_all | solution.py:377
  38.6 0.0 copy-done.14
  38.7 0.6 shard_map.89.rest_ref
  39.3 0.0 copy-start.5
  39.3 0.8 copy-done.5
  40.1 13.9 %all-to-all-done.got_ref = f32[16,40,128]{2,1,0:T(8,128)S(1)} async-done(((f32[16,40,128]{2,1,0:T(8,128)}), f32[16,40,128]{2,1,0:T(8,128)S(1)}, u32[]{:S(2)}, u32[]{:S(2)}) %all-to-all-start) | async-done | bytes 327712 | tf_op jit(solution)/shard_map/all_to_all | solution.py:377
  54.0 2.1 %shard_map.90 = (f32[32,64,128]{2,1,0:T(8,128)}, f32[8,128]{1,0:T(8,128)S(1)}) custom-call(s32[1]{0:T(128)} %bitcast.place_ref, f32[16,40,128]{2,1,0:T(8,128)S(1)} %all-to-all-done.got_ref, f32[32,32,128]{2,1,0:T(8,128)} %copy-done.5), custom_call_target="tpu_custom_call" | custom-call | flops 100000000 | bytes 1048576 | tf_op jit(solution)/shard_map/pallas_call | solution.py:308
  56.0 4.0 %all-to-all-start.2 = ((f32[32,64,128]{2,1,0:T(8,128)}), f32[32,64,128]{2,1,0:T(8,128)S(1)}, u32[]{:S(2)}, u32[]{:S(2)}) async-start(f32[32,64,128]{2,1,0:T(8,128)} %get-tuple-element.18), calls=%async_computation.2 | async-start | bytes 2097152 | tf_op jit(solution)/shard_map/all_to_all | solution.py:345
  60.0 1.3 collective-permute-start
  61.3 0.1 fusion.2.within_ref
  61.5 27.9 %collective-permute-done.low_ref = f32[17,32,128]{2,1,0:T(8,128)S(1)} collective-permute-done((f32[17,32,128]{2,1,0:T(8,128)S(1)}, f32[17,32,128]{2,1,0:T(8,128)S(1)}, u32[]{:S(2)}, u32[]{:S(2)}) %collective-permute-start) | collective-permute-done | bytes 278560 | tf_op jit(solution)/shard_map/ppermute | solution.py:374
  89.3 0.0 copy-done.4
  89.3 1.0 copy-done.6
  90.4 0.9 copy-done.11
  91.3 3.1 %shard_map.87.block_hbm.block_ref = f32[512,896]{1,0:T(8,128)S(1)} custom-call(s32[1]{0:T(128)} %bitcast.place_ref, f32[512,256]{1,0:T(8,128)S(1)} %copy-done.6, f32[256,256]{1,0:T(8,128)S(1)} %bitcast.18, f32[512,512]{1,0:T(8,128)S(1)} %get-tuple-element.15.feat_k.feat_hbm, f32[512,256]{1,0:T(8,128)S(1)} %copy-done.4, ...), custom_call_target="tpu_custom_call" | custom-call | flops 2000000000 | bytes 1048576 | tf_op jit(solution)/shard_map/pallas_call | solution.py:308
  94.5 0.0 copy-start.8
  94.5 0.7 copy-done.8
  95.2 1.2 copy-done.12
  96.4 0.0 all-to-all-done.2.got_ref
  96.4 5.3 %shard_map.91 = (f32[3,512,384]{2,1,0:T(8,128)}, f32[32,40,128]{2,1,0:T(8,128)}) custom-call(s32[32]{0:T(128)S(1)} %fusion.2.within_ref, f32[32,64,128]{2,1,0:T(8,128)S(1)} %all-to-all-done.2.got_ref, f32[8,128]{1,0:T(8,128)S(1)} %get-tuple-element.19.norm_ref, f32[512,896]{1,0:T(8,128)} %copy-done.12), custom_call_target="tpu_custom_call" | custom-call | flops 1000000000 | bytes 1048576 | tf_op jit(solution)/shard_map/pallas_call | solution.py:308
  101.7 0.0 copy-start.9
  101.7 10.1 %all-to-all-start.3 = ((f32[32,40,128]{2,1,0:T(8,128)}), f32[32,40,128]{2,1,0:T(8,128)}, u32[]{:S(2)}, u32[]{:S(2)}) async-start(f32[32,40,128]{2,1,0:T(8,128)} %get-tuple-element.22), calls=%async_computation.3 | async-start | bytes 1310720 | tf_op jit(solution)/shard_map/all_to_all | solution.py:345
  111.8 1.2 slice_bitcast_fusion.grad_ref
  113.0 0.0 copy-done
  113.0 0.0 copy-done.9
  113.0 0.0 copy-start.7
  113.1 1.0 copy-done.7
  114.1 1.5 copy-done.13
  115.6 3.2 %shard_map.92 = (f32[32,16,128]{2,1,0:T(8,128)S(1)}, f32[512,512]{1,0:T(8,128)S(1)}) custom-call(s32[1]{0:T(128)} %bitcast.place_ref, f32[512,256]{1,0:T(8,128)S(1)} %copy-done.7, f32[512,256]{1,0:T(8,128)S(1)} %copy-done.4, f32[512,896]{1,0:T(8,128)S(1)} %copy-done.13, f32[512,512]{1,0:T(8,128)S(1)} %get-tuple-element.15.feat_k.feat_hbm, ...), custom_call_target="tpu_custom_call" | custom-call | flops 4000000000 | bytes 1048576 | tf_op jit(solution)/shard_map/pallas_call | solution.py:308
  118.8 1.0 copy-done.1
  119.8 12.3 %all-to-all-done.3.got_ref = f32[32,40,128]{2,1,0:T(8,128)} async-done(((f32[32,40,128]{2,1,0:T(8,128)}), f32[32,40,128]{2,1,0:T(8,128)}, u32[]{:S(2)}, u32[]{:S(2)}) %all-to-all-start.3) | async-done | bytes 655392 | tf_op jit(solution)/shard_map/all_to_all | solution.py:345
  132.1 2.1 %shard_map.93 = (f32[32,48,128]{2,1,0:T(8,128)}, f32[8,128]{1,0:T(8,128)S(1)}) custom-call(s32[1]{0:T(128)} %bitcast.place_ref, f32[32,40,128]{2,1,0:T(8,128)} %all-to-all-done.3.got_ref, f32[32,16,128]{2,1,0:T(8,128)S(1)} %get-tuple-element.23.rest_ref), custom_call_target="tpu_custom_call" | custom-call | flops 100000000 | bytes 1048576 | tf_op jit(solution)/shard_map/pallas_call | solution.py:308
  134.1 27.7 %all_to_all.30.got_ref = f32[32,48,128]{2,1,0:T(8,128)} all-to-all(f32[32,48,128]{2,1,0:T(8,128)} %get-tuple-element.24), channel_id=1, replica_groups=mesh['seq'=32,'head'=16] {'seq'}, dimensions={0} | all-to-all | bytes 1572864 | tf_op jit(solution)/shard_map/all_to_all | solution.py:345
  161.8 4.3 %shard_map.94 = (f32[32,16,128]{2,1,0:T(8,128)S(1)}, f32[8,256]{1,0:T(8,128)}) custom-call(f32[512,256]{1,0:T(8,128)} %keys_hbm.1, f32[512,256]{1,0:T(8,128)} %values.7, f32[512,512]{1,0:T(8,128)} %copy-done, f32[512,512]{1,0:T(8,128)} %copy-done.1, f32[32,48,128]{2,1,0:T(8,128)} %all_to_all.30.got_ref, f32[8,128]{1,0:T(8,128)S(1)} %get-tuple-element.25.norm_ref), custom_call_target="tpu_custom_call" | custom-call | flops 1000000000 | bytes 1048576 | tf_op jit(solution)/shard_map/pallas_call | solution.py:308
  166.1 16.2 %all_to_all.31.got_ref = f32[32,16,128]{2,1,0:T(8,128)S(1)} all-to-all(f32[32,16,128]{2,1,0:T(8,128)S(1)} %get-tuple-element.27), channel_id=1, replica_groups=mesh['seq'=32,'head'=16] {'seq'}, dimensions={0} | all-to-all | bytes 524288 | tf_op jit(solution)/shard_map/all_to_all | solution.py:345
  182.4 0.6 shard_map.95
  (10 shorter events, 0.0 us)
Async XLA Ops:
  2.6 24.1 %all-to-all-start.1 = ((f32[16,32,256]{2,1,0:T(8,128)}), f32[16,32,256]{2,1,0:T(8,128)S(1)}, u32[]{:S(2)}, u32[]{:S(2)}) async-start(f32[16,32,256]{2,1,0:T(8,128)} %cut.1), calls=%async_computation.1 | async-start | bytes 1048576 | tf_op jit(solution)/shard_map/all_to_all | solution.py:345
  9.8 1.0 copy-start.2
  10.9 1.0 copy-start.3
  11.9 0.9 copy-start.10
  12.9 25.8 %copy-start.14 = (s32[32,32]{1,0:T(8,128)S(1)}, s32[32,32]{1,0:T(8,128)}, u32[]{:S(2)}) copy-start(s32[32,32]{1,0:T(8,128)} %param.13) | copy-start | bytes 12292
  15.0 98.0 %copy-start = (f32[512,512]{1,0:T(8,128)}, f32[512,512]{1,0:T(8,128)S(1)}, u32[]{:S(2)}) copy-start(f32[512,512]{1,0:T(8,128)S(1)} %get-tuple-element.15.feat_k.feat_hbm) | copy-start | bytes 3145732
  15.0 10.9 %collective-permute-start.1 = (f32[17,32,128]{2,1,0:T(8,128)S(1)}, f32[17,32,128]{2,1,0:T(8,128)S(1)}, u32[]{:S(2)}, u32[]{:S(2)}) collective-permute-start(f32[17,32,128]{2,1,0:T(8,128)S(1)} %get-tuple-element.17), channel_id=1, source_target_pairs={{0,16},{16,0},{32,48},{48,32},{64,80},{80,64},{96,112},{112,96},{1... | collective-permute-start | bytes 835592 | tf_op jit(solution)/shard_map/ppermute | solution.py:373
  26.7 27.3 %all-to-all-start = ((f32[16,40,128]{2,1,0:T(8,128)}), f32[16,40,128]{2,1,0:T(8,128)S(1)}, u32[]{:S(2)}, u32[]{:S(2)}) async-start(f32[16,40,128]{2,1,0:T(8,128)} %shard_map.88), calls=%async_computation | async-start | bytes 655360 | tf_op jit(solution)/shard_map/all_to_all | solution.py:377
  39.3 0.8 copy-start.5
  40.1 49.3 %copy-start.4 = (f32[512,256]{1,0:T(8,128)S(1)}, f32[512,256]{1,0:T(8,128)}, u32[]{:S(2)}) copy-start(f32[512,256]{1,0:T(8,128)} %values.7) | copy-start | bytes 1572868
  56.0 40.4 %all-to-all-start.2 = ((f32[32,64,128]{2,1,0:T(8,128)}), f32[32,64,128]{2,1,0:T(8,128)S(1)}, u32[]{:S(2)}, u32[]{:S(2)}) async-start(f32[32,64,128]{2,1,0:T(8,128)} %get-tuple-element.18), calls=%async_computation.2 | async-start | bytes 2097152 | tf_op jit(solution)/shard_map/all_to_all | solution.py:345
  60.0 29.3 %collective-permute-start = (f32[17,32,128]{2,1,0:T(8,128)S(1)}, f32[17,32,128]{2,1,0:T(8,128)S(1)}, u32[]{:S(2)}, u32[]{:S(2)}) collective-permute-start(f32[17,32,128]{2,1,0:T(8,128)S(1)} %get-tuple-element.16.keep_ref), channel_id=1, source_target_pairs={{0,16},{32,48},{64,80},{96,112},{128,144},{160,176},{192,208},{224... | collective-permute-start | bytes 835592 | tf_op jit(solution)/shard_map/ppermute | solution.py:374
  89.3 1.0 copy-start.6
  90.4 0.9 copy-start.11
  94.5 0.7 copy-start.8
  95.2 1.2 copy-start.12
  101.7 11.4 %copy-start.9 = (f32[17,32,128]{2,1,0:T(8,128)S(1)}, f32[17,32,128]{2,1,0:T(8,128)}, u32[]{:S(2)}) copy-start(f32[17,32,128]{2,1,0:T(8,128)} %copy-done.8) | copy-start | bytes 835588
  101.7 30.4 %all-to-all-start.3 = ((f32[32,40,128]{2,1,0:T(8,128)}), f32[32,40,128]{2,1,0:T(8,128)}, u32[]{:S(2)}, u32[]{:S(2)}) async-start(f32[32,40,128]{2,1,0:T(8,128)} %get-tuple-element.22), calls=%async_computation.3 | async-start | bytes 1310720 | tf_op jit(solution)/shard_map/all_to_all | solution.py:345
  113.0 1.0 copy-start.7
  114.1 1.5 copy-start.13
  118.8 1.0 copy-start.1

commit v6 on v4

--- a/solution.py
+++ b/solution.py
@@ -174,7 +174,7 @@
             out_ref[owner, base : base + rows, :] = blocks_ref[place, :, c * LANES : (c + 1) * LANES]
 
 
-def backward_scan_kernel(state_rows, place_ref, got_ref, term_ref, out_ref, norm_ref):
+def backward_scan_kernel(state_rows, place_ref, got_ref, out_ref, norm_ref):
     mine = place_ref[0]
     total = jnp.zeros((state_rows, LANES), jnp.float32)
     norm = jnp.zeros((ROWS, LANES), jnp.float32)
@@ -183,7 +183,6 @@
         total = total + got_ref[place, :state_rows, :]
         norm = norm + jnp.where(place > mine, got_ref[place, state_rows:, :], 0.0)
     norm_ref[...] = norm
-    out_ref[:, state_rows:, :] = term_ref[...]
 
 
 def norm_row(norm_ref, count):
@@ -262,17 +261,22 @@
     pack(term_ref, 0, dot3(halves(queries[...]), halves(pre_ref[...]), TN))
 
 
-def close_kernel(keys, values, feat_k, inner, got_ref, norm_ref, term_ref, query_ref):
+def close_kernel(keys, values, feat_k, inner, got_ref, norm_ref, query_ref, term_ref):
     feats = feat_k.shape[1]
     chunks = feats // LANES
     state = unpack(got_ref, 0, chunks)
     grad_fk = inner[...] + dot3(halves(values[...]), halves(state), NN) + norm_row(norm_ref, chunks)
     grad_pk = back_pair(feat_k[...], grad_fk, feats // 2)
     pack(term_ref, 0, dot3(halves(keys[...]), halves(grad_pk), TN))
-    sum_kernel(chunks * ROWS, got_ref, query_ref)
-
-
-def sum_kernel(base, got_ref, out_ref):
+    term_ref[:, query_ref.shape[1] :, :] = query_ref[...]
+
+
+def sum_kernel(got_ref, key_ref, query_ref):
+    sum_slices(0, got_ref, key_ref)
+    sum_slices(got_ref.shape[1] // 2, got_ref, query_ref)
+
+
+def sum_slices(base, got_ref, out_ref):
     for c in range(out_ref.shape[1] // LANES):
         part = got_ref[:, base + c * ROWS : base + (c + 1) * ROWS, :]
         out_ref[:, c * LANES : (c + 1) * LANES] = jnp.sum(part, axis=0)
@@ -374,16 +378,16 @@
     )
     out4, next_norm = call(
         functools.partial(backward_scan_kernel, state_rows),
-        [(count, state_rows + term_rows, LANES), (ROWS, LANES)],
-        "svv", 0.1, (place, got3, term_q),
+        [(count, state_rows, LANES), (ROWS, LANES)],
+        "sv", 0.1, (place, got3),
     )
     got4 = exchange(out4, "seq")
-    out5, grad_query = call(
-        close_kernel, [(count, term_rows, LANES), (width // count, half)], "vvvvvv", 1.0,
-        (keys, values, feat_k, inner, got4, next_norm),
+    (out5,) = call(
+        close_kernel, [(count, 2 * term_rows, LANES)], "vvvvvvv", 1.0,
+        (keys, values, feat_k, inner, got4, next_norm, term_q),
     )
     got5 = exchange(out5, "seq")
-    (grad_key,) = call(functools.partial(sum_kernel, 0), [(width // count, half)], "v", 0.1, (got5,))
+    grad_key, grad_query = call(sum_kernel, [(width // count, half)] * 2, "v", 0.1, (got5,))
     return (grad_query[None], grad_key[None])
 
 

time: 194 us -> 194 us (level)
  blocking collectives: 44.1 us -> 53.2 us
  starting transfers between devices: 41.6 us -> 35.5 us
  waiting for transfers between devices: 70 us -> 66.4 us
    all_to_all x2, blocking collectives: 44.1 us -> 53.2 us  [exchange(): return lax.all_to_all(value, axis, split_axis=0, concat_axis=0, tiled=True)]
    all_to_all x3, starting transfers between devices: 22.6 us -> 16.4 us  [exchange(): return lax.all_to_all(value, axis, split_axis=0, concat_axis=0, tiled=True)]
    all_to_all x3, waiting for transfers between devices: 26.1 us -> 22.5 us  [exchange(): return lax.all_to_all(value, axis, split_axis=0, concat_axis=0, tiled=True)]
    unnamed x46 -> x44, local copies, waits for them, and re-layouts: 17.1 us -> 18.5 us
where the time goes in v6:
time: 194 us; the launch traced here: 193 us
  waiting for transfers between devices  66.4 us (34%)
  blocking collectives  53.2 us (27%)
  starting transfers between devices  35.5 us (18%)
  local copies, waits for them, and re-layouts  18.5 us (10%)
  Pallas kernels  18.1 us (9%)
    all_to_all x2, blocking collectives, exchange(): return lax.all_to_all(value, axis, split_axis=0, concat_axis=0, tiled=True)  53.2 us
    ppermute x1, waiting for transfers between devices, per_device(): given = lax.ppermute(keep, 'seq', [(s, s + 1) for s in range(0, count, 2)])  27.9 us
    all_to_all x3, waiting for transfers between devices, exchange(): return lax.all_to_all(value, axis, split_axis=0, concat_axis=0, tiled=True)  22.5 us
    unnamed x44, local copies, waits for them, and re-layouts  18.5 us
    all_to_all x3, starting transfers between devices, exchange(): return lax.all_to_all(value, axis, split_axis=0, concat_axis=0, tiled=True)  16.4 us
    pallas_call x9, Pallas kernels, call(): pl.pallas_call(body, out_shape=[jax.ShapeDtypeStruct(shape, jnp.float32)...  16.2 us
    all_to_all x1, waiting for transfers between devices, per_device(): lax.all_to_all(out1, 'seq', split_axis=0, concat_axis=0, axis_index_group...  11.6 us
    all_to_all x1, starting transfers between devices, per_device(): lax.all_to_all(out1, 'seq', split_axis=0, concat_axis=0, axis_index_group...  10.8 us
  transfers between devices with their start and end apart: 6, of which 5 were waited for; matrix products, arithmetic and copies ran while one was open for 0% of the time, Pallas kernels for 4%

profile of v6, /device:TPU:64, one launch (start us, length us, event | category | flops | bytes accessed | tf_op | source)
XLA Modules:
  0.0 192.6 jit_solution(263023471603864529)
XLA Ops:
  0.6 0.0 copy-start.2
  0.6 1.0 copy-done.2
  1.7 1.0 copy-done.4
  2.7 0.9 copy-done.14
  3.7 2.2 %shard_map.86 = (f32[512,512]{1,0:T(8,128)S(1)}, f32[17,32,128]{2,1,0:T(8,128)S(1)}, f32[17,32,128]{2,1,0:T(8,128)S(1)}) custom-call(s32[1]{0:T(128)} %bitcast.place_ref, f32[512,256]{1,0:T(8,128)S(1)} %copy-done.2, f32[256,256]{1,0:T(8,128)S(1)} %bitcast.15, f32[512,256]{1,0:T(8,128)S(1)} %copy-done.4), custom_call_target="tpu_custom_call" | custom-call | flops 1000000000 | bytes 1048576 | tf_op jit(solution)/shard_map/pallas_call | solution.py:288
  5.8 0.0 copy-start.21
  5.9 6.9 %collective-permute-start.1 = (f32[17,32,128]{2,1,0:T(8,128)S(1)}, f32[17,32,128]{2,1,0:T(8,128)S(1)}, u32[]{:S(2)}, u32[]{:S(2)}) collective-permute-start(f32[17,32,128]{2,1,0:T(8,128)S(1)} %get-tuple-element.17), channel_id=1, source_target_pairs={{0,16},{16,0},{32,48},{48,32},{64,80},{80,64},{96,112},{112,96},{1... | collective-permute-start | bytes 835592 | tf_op jit(solution)/shard_map/ppermute | solution.py:352
  12.8 4.5 %collective-permute-done.1.high_ref.got_ref = f32[17,32,128]{2,1,0:T(8,128)S(1)} collective-permute-done((f32[17,32,128]{2,1,0:T(8,128)S(1)}, f32[17,32,128]{2,1,0:T(8,128)S(1)}, u32[]{:S(2)}, u32[]{:S(2)}) %collective-permute-start.1) | collective-permute-done | bytes 278560 | tf_op jit(solution)/shard_map/ppermute | solution.py:352
  17.3 0.8 shard_map.88
  18.0 10.8 %all-to-all-start = ((f32[16,40,128]{2,1,0:T(8,128)}), f32[16,40,128]{2,1,0:T(8,128)S(1)}, u32[]{:S(2)}, u32[]{:S(2)}) async-start(f32[16,40,128]{2,1,0:T(8,128)} %shard_map.88), calls=%async_computation | async-start | bytes 655360 | tf_op jit(solution)/shard_map/all_to_all | solution.py:356
  28.9 1.9 %cut.1 = f32[16,32,256]{2,1,0:T(8,128)} custom-call(f32[32,4096]{1,0:T(8,128)} %in_ref.1), custom_call_target="tpu_custom_call" | custom-call | tf_op jit(solution)/shard_map/cut/pallas_call | solution.py:313
  30.8 0.0 copy-start.5
  30.8 11.6 %all-to-all-done.got_ref = f32[16,40,128]{2,1,0:T(8,128)S(1)} async-done(((f32[16,40,128]{2,1,0:T(8,128)}), f32[16,40,128]{2,1,0:T(8,128)S(1)}, u32[]{:S(2)}, u32[]{:S(2)}) %all-to-all-start) | async-done | bytes 327712 | tf_op jit(solution)/shard_map/all_to_all | solution.py:356
  42.4 7.2 %all-to-all-start.1 = ((f32[16,32,256]{2,1,0:T(8,128)}), f32[16,32,256]{2,1,0:T(8,128)S(1)}, u32[]{:S(2)}, u32[]{:S(2)}) async-start(f32[16,32,256]{2,1,0:T(8,128)} %cut.1), calls=%async_computation.1 | async-start | bytes 1048576 | tf_op jit(solution)/shard_map/all_to_all | solution.py:324
  49.7 15.9 %all-to-all-done.1 = f32[16,32,256]{2,1,0:T(8,128)S(1)} async-done(((f32[16,32,256]{2,1,0:T(8,128)}), f32[16,32,256]{2,1,0:T(8,128)S(1)}, u32[]{:S(2)}, u32[]{:S(2)}) %all-to-all-start.1) | async-done | bytes 524320 | tf_op jit(solution)/shard_map/all_to_all | solution.py:324
  65.6 1.6 shard_map.89
  67.2 4.3 %all-to-all-start.2 = ((f32[32,64,128]{2,1,0:T(8,128)}), f32[32,64,128]{2,1,0:T(8,128)S(1)}, u32[]{:S(2)}, u32[]{:S(2)}) async-start(f32[32,64,128]{2,1,0:T(8,128)} %get-tuple-element.18), calls=%async_computation.2 | async-start | bytes 2097152 | tf_op jit(solution)/shard_map/all_to_all | solution.py:324
  71.5 1.3 collective-permute-start
  72.8 0.1 fusion.2.within_ref
  72.9 27.9 %collective-permute-done.low_ref = f32[17,32,128]{2,1,0:T(8,128)S(1)} collective-permute-done((f32[17,32,128]{2,1,0:T(8,128)S(1)}, f32[17,32,128]{2,1,0:T(8,128)S(1)}, u32[]{:S(2)}, u32[]{:S(2)}) %collective-permute-start) | collective-permute-done | bytes 278560 | tf_op jit(solution)/shard_map/ppermute | solution.py:353
  100.7 1.0 copy-done.10
  101.8 0.9 copy-done.15
  102.7 3.1 %shard_map.87.block_ref = f32[512,896]{1,0:T(8,128)S(1)} custom-call(s32[1]{0:T(128)} %bitcast.place_ref, f32[512,256]{1,0:T(8,128)S(1)} %copy-done.10, f32[256,256]{1,0:T(8,128)S(1)} %bitcast.16, f32[512,512]{1,0:T(8,128)S(1)} %get-tuple-element.15.feat_k, f32[512,256]{1,0:T(8,128)S(1)} %copy-done.5, f32[17,32,128]{2,1,0:T(8,128)S(1)} %collective-permute-done.low_ref, ...), custom_call_target="tpu_custom_call" | custom-call | flops 2000000000 | bytes 1048576 | tf_op jit(solution)/shard_map/pallas_call | solution.py:288
  105.9 0.7 copy-done.12
  106.6 1.3 copy-done.16
  107.8 0.0 all-to-all-done.2.got_ref
  107.8 1.9 copy-done.17
  109.7 2.5 %shard_map.90 = (f32[512,384]{1,0:T(8,128)S(1)}, f32[32,40,128]{2,1,0:T(8,128)S(1)}) custom-call(s32[32]{0:T(128)S(1)} %fusion.2.within_ref, f32[32,64,128]{2,1,0:T(8,128)S(1)} %all-to-all-done.2.got_ref, f32[8,128]{1,0:T(8,128)S(1)} %get-tuple-element.19.norm_ref, f32[512,896]{1,0:T(8,128)S(1)} %copy-done.17), custom_call_target="tpu_custom_call" | custom-call | flops 1000000000 | bytes 1048576 | tf_op jit(solution)/shard_map/pallas_call | solution.py:288
  112.2 0.0 copy-done
  112.2 0.0 copy-start.19
  112.3 31.5 %all_to_all.30.got_ref = f32[32,40,128]{2,1,0:T(8,128)S(1)} all-to-all(f32[32,40,128]{2,1,0:T(8,128)S(1)} %get-tuple-element.22), channel_id=1, replica_groups=mesh['seq'=32,'head'=16] {'seq'}, dimensions={0} | all-to-all | bytes 1310720 | tf_op jit(solution)/shard_map/all_to_all | solution.py:324
  143.8 0.8 shard_map.92
  144.6 5.0 %all-to-all-start.4 = ((f32[32,32,128]{2,1,0:T(8,128)}), f32[32,32,128]{2,1,0:T(8,128)S(1)}, u32[]{:S(2)}, u32[]{:S(2)}) async-start(f32[32,32,128]{2,1,0:T(8,128)} %get-tuple-element.23), calls=%async_computation.4 | async-start | bytes 1048576 | tf_op jit(solution)/shard_map/all_to_all | solution.py:324
  149.6 0.0 copy-start.1
  149.6 1.2 copy-done.1
  150.9 1.0 copy-done.6
  151.9 1.0 copy-done.11
  152.9 1.0 copy-done.13
  153.9 1.5 copy-done.18
  155.4 1.1 copy-done.20
  156.5 3.2 %shard_map.91 = (f32[32,16,128]{2,1,0:T(8,128)S(1)}, f32[512,512]{1,0:T(8,128)S(1)}) custom-call(s32[1]{0:T(128)} %bitcast.place_ref, f32[512,256]{1,0:T(8,128)S(1)} %copy-done.11, f32[512,256]{1,0:T(8,128)S(1)} %copy-done.6, f32[512,896]{1,0:T(8,128)S(1)} %copy-done.18, f32[512,512]{1,0:T(8,128)S(1)} %get-tuple-element.15.feat_k, ...), custom_call_target="tpu_custom_call" | custom-call | flops 4000000000 | bytes 1048576 | tf_op jit(solution)/shard_map/pallas_call | solution.py:288
  159.7 0.7 copy-done.8
  160.4 6.5 %all-to-all-done.4.got_ref = f32[32,32,128]{2,1,0:T(8,128)S(1)} async-done(((f32[32,32,128]{2,1,0:T(8,128)}), f32[32,32,128]{2,1,0:T(8,128)S(1)}, u32[]{:S(2)}, u32[]{:S(2)}) %all-to-all-start.4) | async-done | bytes 524320 | tf_op jit(solution)/shard_map/all_to_all | solution.py:324
  167.0 1.0 copy-done.7
  168.0 0.9 copy-done.9
  169.0 1.4 shard_map.93
  170.3 21.7 %all_to_all.31.got_ref = f32[32,32,128]{2,1,0:T(8,128)S(1)} all-to-all(f32[32,32,128]{2,1,0:T(8,128)S(1)} %shard_map.93), channel_id=1, replica_groups=mesh['seq'=32,'head'=16] {'seq'}, dimensions={0} | all-to-all | bytes 1048576 | tf_op jit(solution)/shard_map/all_to_all | solution.py:324
  192.0 0.6 shard_map.94
  (22 shorter events, 0.1 us)
Async XLA Ops:
  0.6 1.0 copy-start.2
  1.7 1.0 copy-start.4
  2.7 0.9 copy-start.14
  5.8 43.8 %copy-start.21 = (s32[32,32]{1,0:T(8,128)S(1)}, s32[32,32]{1,0:T(8,128)}, u32[]{:S(2)}) copy-start(s32[32,32]{1,0:T(8,128)} %param.13) | copy-start | bytes 12292
  5.9 11.4 %collective-permute-start.1 = (f32[17,32,128]{2,1,0:T(8,128)S(1)}, f32[17,32,128]{2,1,0:T(8,128)S(1)}, u32[]{:S(2)}, u32[]{:S(2)}) collective-permute-start(f32[17,32,128]{2,1,0:T(8,128)S(1)} %get-tuple-element.17), channel_id=1, source_target_pairs={{0,16},{16,0},{32,48},{48,32},{64,80},{80,64},{96,112},{112,96},{1... | collective-permute-start | bytes 835592 | tf_op jit(solution)/shard_map/ppermute | solution.py:352
  18.0 24.4 %all-to-all-start = ((f32[16,40,128]{2,1,0:T(8,128)}), f32[16,40,128]{2,1,0:T(8,128)S(1)}, u32[]{:S(2)}, u32[]{:S(2)}) async-start(f32[16,40,128]{2,1,0:T(8,128)} %shard_map.88), calls=%async_computation | async-start | bytes 655360 | tf_op jit(solution)/shard_map/all_to_all | solution.py:356
  30.8 69.9 %copy-start.5 = (f32[512,256]{1,0:T(8,128)S(1)}, f32[512,256]{1,0:T(8,128)}, u32[]{:S(2)}) copy-start(f32[512,256]{1,0:T(8,128)} %values.7) | copy-start | bytes 1572868
  42.4 23.1 %all-to-all-start.1 = ((f32[16,32,256]{2,1,0:T(8,128)}), f32[16,32,256]{2,1,0:T(8,128)S(1)}, u32[]{:S(2)}, u32[]{:S(2)}) async-start(f32[16,32,256]{2,1,0:T(8,128)} %cut.1), calls=%async_computation.1 | async-start | bytes 1048576 | tf_op jit(solution)/shard_map/all_to_all | solution.py:324
  67.2 40.6 %all-to-all-start.2 = ((f32[32,64,128]{2,1,0:T(8,128)}), f32[32,64,128]{2,1,0:T(8,128)S(1)}, u32[]{:S(2)}, u32[]{:S(2)}) async-start(f32[32,64,128]{2,1,0:T(8,128)} %get-tuple-element.18), calls=%async_computation.2 | async-start | bytes 2097152 | tf_op jit(solution)/shard_map/all_to_all | solution.py:324
  71.5 29.3 %collective-permute-start = (f32[17,32,128]{2,1,0:T(8,128)S(1)}, f32[17,32,128]{2,1,0:T(8,128)S(1)}, u32[]{:S(2)}, u32[]{:S(2)}) collective-permute-start(f32[17,32,128]{2,1,0:T(8,128)S(1)} %get-tuple-element.16.keep_ref), channel_id=1, source_target_pairs={{0,16},{32,48},{64,80},{96,112},{128,144},{160,176},{192,208},{224... | collective-permute-start | bytes 835592 | tf_op jit(solution)/shard_map/ppermute | solution.py:353
  100.7 1.0 copy-start.10
  101.8 0.9 copy-start.15
  105.9 0.7 copy-start.12
  106.6 1.3 copy-start.16
  107.8 4.4 %copy-start = (f32[32,64,128]{2,1,0:T(8,128)}, f32[32,64,128]{2,1,0:T(8,128)S(1)}, u32[]{:S(2)}) copy-start(f32[32,64,128]{2,1,0:T(8,128)S(1)} %all-to-all-done.2.got_ref) | copy-start | bytes 3145732
  107.8 1.9 copy-start.17
  112.2 32.4 %copy-start.19 = (f32[512,384]{1,0:T(8,128)}, f32[512,384]{1,0:T(8,128)S(1)}, u32[]{:S(2)}) copy-start(f32[512,384]{1,0:T(8,128)S(1)} %get-tuple-element.20.grad_ref) | copy-start | bytes 2359300
  144.6 22.3 %all-to-all-start.4 = ((f32[32,32,128]{2,1,0:T(8,128)}), f32[32,32,128]{2,1,0:T(8,128)S(1)}, u32[]{:S(2)}, u32[]{:S(2)}) async-start(f32[32,32,128]{2,1,0:T(8,128)} %get-tuple-element.23), calls=%async_computation.4 | async-start | bytes 1048576 | tf_op jit(solution)/shard_map/all_to_all | solution.py:324
  149.6 1.2 copy-start.1
  150.9 1.0 copy-start.6
  151.9 1.0 copy-start.11
  152.9 1.0 copy-start.13
  153.9 1.5 copy-start.18
  155.4 1.1 copy-start.20
  156.5 10.4 %copy-start.3 = (f32[512,256]{1,0:T(8,128)S(1)}, f32[512,256]{1,0:T(8,128)}, u32[]{:S(2)}) copy-start(f32[512,256]{1,0:T(8,128)} %keys.3) | copy-start | bytes 1572868
  159.7 0.7 copy-start.8
  167.0 1.0 copy-start.7
  168.0 0.9 copy-start.9
